TPU v7x, 32 devices: a whole 2x2x4 slice. The times are simulated.
32 devices in a mesh: depth: 8 (over z, y), xline: 4 (over x, core).
Axes of the slice: x: 2, y: 2, z: 4, core: 2. Of those that a mesh axis runs over, the one named last changes fastest.
Arguments:
- surface_fields: float32 [2, 2, 2, 64, 128], P(None, None, None, 'xline'), may hold values from -6 to 6
- stencil_table: float32 [13, 2, 2, 128], replicated
- velocity_bins: int32 [8, 2, 64, 128], P('depth', None, 'xline'), may hold values from 0 to 127
- offset_list: int32 [16, 2], replicated, may hold values from -8 to 8, as said below
Outputs:
- image_tiles: float32 [8, 16, 64, 128], P('depth', None, 'xline')
Inputs may be any that keep to these rules, and one draw needn't show every extreme that they name: `offset_list`: column 0 lies within -8 to 8 and column 1 within -8 to 8; both ends of both ranges occur in every draw.
All inputs are finite; a program needn't handle non-finite values.
Results may differ from a plain program's by a relative error of at most 0.0003.
Values sent between devices are 32-bit elements; how exact they have to be, the bound alone decides.
No kernel may reach another device: no remote copies, remote signals or barrier semaphores. Data moves between devices by JAX's collectives and lax.ppermute only.
A program may use at most 64 MiB of HBM per device.

v0:
```python
import jax
import jax.numpy as jnp
from jax import lax
from jax.sharding import PartitionSpec as P

OFF_Y = 8
OFF_X = 8


tap_rows = (0, -4, -3, -2, -1, 1, 2, 3, 4, 0, 0, 0, 0)
tap_cols = (0, 0, 0, 0, 0, 0, 0, 0, 0, -2, -1, 1, 2)
reach_rows = 4
reach_cols = 2


def with_halo(array, sides, width):
    for axis, dim in sides:
        count, length = (lax.axis_size(axis), array.shape[dim])
        up = [(i, (i + 1) % count) for i in range(count - 1)]
        down = [(j, i) for i, j in up]
        last = lax.slice_in_dim(array, length - width, length, axis=dim)
        leading = lax.slice_in_dim(array, 0, width, axis=dim)
        before = lax.ppermute(last, axis, up)
        after = lax.ppermute(leading, axis, down)
        array = jnp.concatenate([before, array, after], axis=dim)
    return array


def shifted_2(block, axis, distance):
    devices = range(lax.axis_size(axis))
    route = [(i - distance, i) for i in devices if i - distance in devices]
    return lax.ppermute(block, axis, route)


def extrapolate(fields, coefficients):
    row_count = fields.shape[3] - 2 * reach_rows
    inline_width = fields.shape[4]
    padded = jnp.pad(fields, ((0, 0), (0, 0), (0, 0), (0, 0), (reach_cols, reach_cols)))
    conj_sign = jnp.array([1.0, -1.0], dtype=jnp.float32).reshape(2, 1, 1, 1)
    real_part = None
    imag_part = None
    for tap_index in range(len(tap_rows)):
        first_row = reach_rows + tap_rows[tap_index]
        first_col = reach_cols + tap_cols[tap_index]
        shifted = padded[
            :, :, :, first_row : first_row + row_count, first_col : first_col + inline_width
        ]
        coef_real = coefficients[tap_index, 0]
        coef_imag = coefficients[tap_index, 1] * conj_sign
        term_real = coef_real * shifted[:, 0] - coef_imag * shifted[:, 1]
        term_imag = coef_real * shifted[:, 1] + coef_imag * shifted[:, 0]
        if tap_index == 0:
            real_part = term_real
            imag_part = term_imag
        else:
            real_part = real_part + term_real
            imag_part = imag_part + term_imag
    return jnp.stack([real_part, imag_part], axis=1)


def correlate(source, receiver, offset_list):
    padded = jnp.pad(receiver, ((0, 0), (0, 0), (0, 0), (OFF_X, OFF_X)))
    slice_shape = (2, source.shape[1], source.shape[2], source.shape[3])

    def one_offset(offset_couple):
        starts = (jnp.int32(0), jnp.int32(0), OFF_Y + offset_couple[0], OFF_X + offset_couple[1])
        shifted = lax.dynamic_slice(padded, starts, slice_shape)
        return jnp.sum(source[0] * shifted[0] + source[1] * shifted[1], axis=0)

    return jax.vmap(one_offset)(offset_list)


def within_mesh(first_row, span_rows, grid_rows):
    row_ids = first_row + jnp.arange(span_rows, dtype=jnp.int32)
    return ((row_ids >= 0) & (row_ids < grid_rows)).astype(jnp.float32)[:, None]


def shards(surface_fields, stencil_table, velocity_bins, offset_list):
    depth_count = lax.axis_size("depth")
    depth_index = lax.axis_index("depth")
    crossline_index = lax.axis_index("xline")
    row_count = surface_fields.shape[3]
    inline_width = surface_fields.shape[4]
    freq_count = surface_fields.shape[2]
    grid_rows = row_count * lax.axis_size("xline")
    base_row = crossline_index * row_count
    group_size = 1
    group_count = freq_count // group_size
    section_count = depth_count + group_count - 1
    slab_velocity = velocity_bins[0]
    margin = reach_rows + OFF_Y
    extended = with_halo(slab_velocity, (("xline", 1),), reach_rows + OFF_Y)
    ext_rows = row_count + 2 * margin
    vel_count = stencil_table.shape[3]
    flat_table = stencil_table.reshape(-1, vel_count)
    bin_ids = jnp.arange(vel_count, dtype=jnp.int32)[:, None]
    level_tables = []
    for level_index in range(velocity_bins.shape[1]):
        onehot = (bin_ids == extended[level_index].reshape(1, -1)).astype(jnp.float32)
        product = jnp.dot(
            flat_table, onehot, precision=lax.Precision.HIGHEST, preferred_element_type=jnp.float32
        )
        level_tables.append(
            product.reshape(stencil_table.shape[0], 2, freq_count, ext_rows, inline_width)
        )
    coefficients = jnp.stack(level_tables)

    def advance(section_index, state_pair):
        outgoing, image_tile = state_pair
        group_index = section_index - depth_index
        active = (group_index >= 0) & (group_index < group_count)
        clipped = jnp.clip(group_index, 0, group_count - 1)
        incoming = shifted_2(outgoing, "depth", 1)
        fresh = lax.dynamic_slice_in_dim(surface_fields, clipped * group_size, group_size, 2)
        fields = jnp.where(depth_index == 0, fresh, incoming)
        level_coefs = lax.dynamic_slice_in_dim(coefficients, clipped * group_size, group_size, 3)
        padded = with_halo(fields, (("xline", 3),), 2 * reach_rows + OFF_Y)
        upper = extrapolate(padded, level_coefs[0]) * within_mesh(
            base_row - margin, ext_rows, grid_rows
        )
        lower_rows = row_count + 2 * OFF_Y
        lower = extrapolate(upper, level_coefs[1][:, :, :, reach_rows : reach_rows + lower_rows])
        lower = lower * within_mesh(base_row - OFF_Y, lower_rows, grid_rows)
        fields = lower[:, :, :, OFF_Y : OFF_Y + row_count]
        receiver = lower[1]
        image_tile = image_tile + jnp.where(
            active, correlate(fields[0], receiver, offset_list), 0.0
        )
        return (fields, image_tile)

    start_fields = jnp.zeros((2, 2, group_size, row_count, inline_width), jnp.float32)
    start_image = jnp.zeros((offset_list.shape[0], row_count, inline_width), jnp.float32)
    final_fields, image_tile = lax.fori_loop(0, section_count, advance, (start_fields, start_image))
    return image_tile[None]


def solution(mesh):
    return jax.shard_map(
        shards,
        mesh=mesh,
        in_specs=(P(None, None, None, "xline", None), P(), P("depth", None, "xline", None), P()),
        out_specs=P("depth", None, "xline", None),
        check_vma=False,
    )
```

profile of v0, /device:TPU:26, one launch (start us, length us, event | category | flops | bytes accessed | tf_op | source)
XLA Modules:
  0.0 437.3 jit_solution(12898106134504602882)
XLA Ops:
  0.8 1.9 collective-permute-start.3
  2.7 3.6 collective-permute-start.4
  11.8 424.8 %while.27 = (s32[]{:T(128)}, f32[2,2,1,16,128]{4,3,1,2,0:T(8,128)S(1)}, f32[16,16,128]{2,1,0:T(8,128)S(1)}, s32[]{:T(128)}, f32[2,13,2,2,40,128]{5,4,3,2,1,0:T(8...) while((s32[]{:T(128)}, ...), condition=%wide.region_1.2_spmd.clone.clone.clone, body=%wide.region_0.1_spmd.sunk.clone.clone.clone.sunk | while | flops 2687603 | bytes 13050807 | solution.py:133
  11.8 3.4 collective-permute-start
  17.0 1.5 collective-permute-done
  19.3 2.5 collective-permute-start.1
  21.8 1.9 collective-permute-start.2
  24.3 2.8 collective-permute-done.2
  29.5 30.0 %while.28 = (s32[]{:T(128)}, f32[2,1,32,144]{3,2,1,0:T(8,128)S(1)}, s32[16,4]{0,1:T(4,128)S(1)}, f32[16,2,1,16,128]{4,3,0,2,1:T(8,128)S(1)}, s32[]{:T(128)}) while((s32[]{:T(128)}, f32[2,1,32,144]{3,2,1,0:T(8,128)S(1)}, s32[16,4]{0,1:T(4,128)S(1)}, f32[16,2,1,16,128]{4,3,0,2,1:T(8,128)S(1)}, s32[]{:T(128)}) %tuple.138), condition=%wide.while_cond, body=%wide.while_body.sunk | while | flops 2 | bytes 32893 | solution.py:67
  33.8 1.3 bitcast_dynamic-update-slice_fusion.2
  35.7 1.3 bitcast_dynamic-update-slice_fusion.2
  41.3 1.3 bitcast_dynamic-update-slice_fusion.2
  43.2 1.3 bitcast_dynamic-update-slice_fusion.2
  48.8 1.3 bitcast_dynamic-update-slice_fusion.2
  50.7 1.3 bitcast_dynamic-update-slice_fusion.2
  54.4 1.3 bitcast_dynamic-update-slice_fusion.2
  59.5 2.5 collective-permute-start
  63.8 2.4 collective-permute-done
  67.0 1.9 collective-permute-start.1
  68.9 2.4 collective-permute-start.2
  71.9 2.3 collective-permute-done.2
  76.6 30.0 %while.28 = (s32[]{:T(128)}, f32[2,1,32,144]{3,2,1,0:T(8,128)S(1)}, s32[16,4]{0,1:T(4,128)S(1)}, f32[16,2,1,16,128]{4,3,0,2,1:T(8,128)S(1)}, s32[]{:T(128)}) while((s32[]{:T(128)}, f32[2,1,32,144]{3,2,1,0:T(8,128)S(1)}, s32[16,4]{0,1:T(4,128)S(1)}, f32[16,2,1,16,128]{4,3,0,2,1:T(8,128)S(1)}, s32[]{:T(128)}) %tuple.138), condition=%wide.while_cond, body=%wide.while_body.sunk | while | flops 2 | bytes 32893 | solution.py:67
  106.7 1.9 collective-permute-start
  110.3 3.1 collective-permute-done
  114.1 1.9 collective-permute-start.1
  116.1 2.4 collective-permute-start.2
  119.1 2.3 collective-permute-done.2
  123.8 30.0 %while.28 = (s32[]{:T(128)}, f32[2,1,32,144]{3,2,1,0:T(8,128)S(1)}, s32[16,4]{0,1:T(4,128)S(1)}, f32[16,2,1,16,128]{4,3,0,2,1:T(8,128)S(1)}, s32[]{:T(128)}) while((s32[]{:T(128)}, f32[2,1,32,144]{3,2,1,0:T(8,128)S(1)}, s32[16,4]{0,1:T(4,128)S(1)}, f32[16,2,1,16,128]{4,3,0,2,1:T(8,128)S(1)}, s32[]{:T(128)}) %tuple.138), condition=%wide.while_cond, body=%wide.while_body.sunk | while | flops 2 | bytes 32893 | solution.py:67
  153.8 1.9 collective-permute-start
  157.5 3.1 collective-permute-done
  161.3 1.9 collective-permute-start.1
  163.2 2.4 collective-permute-start.2
  166.2 2.3 collective-permute-done.2
  170.9 30.0 %while.28 = (s32[]{:T(128)}, f32[2,1,32,144]{3,2,1,0:T(8,128)S(1)}, s32[16,4]{0,1:T(4,128)S(1)}, f32[16,2,1,16,128]{4,3,0,2,1:T(8,128)S(1)}, s32[]{:T(128)}) while((s32[]{:T(128)}, f32[2,1,32,144]{3,2,1,0:T(8,128)S(1)}, s32[16,4]{0,1:T(4,128)S(1)}, f32[16,2,1,16,128]{4,3,0,2,1:T(8,128)S(1)}, s32[]{:T(128)}) %tuple.138), condition=%wide.while_cond, body=%wide.while_body.sunk | while | flops 2 | bytes 32893 | solution.py:67
  201.0 1.9 collective-permute-start
  204.6 3.1 collective-permute-done
  208.4 1.9 collective-permute-start.1
  210.3 2.4 collective-permute-start.2
  213.4 2.3 collective-permute-done.2
  218.0 30.0 %while.28 = (s32[]{:T(128)}, f32[2,1,32,144]{3,2,1,0:T(8,128)S(1)}, s32[16,4]{0,1:T(4,128)S(1)}, f32[16,2,1,16,128]{4,3,0,2,1:T(8,128)S(1)}, s32[]{:T(128)}) while((s32[]{:T(128)}, f32[2,1,32,144]{3,2,1,0:T(8,128)S(1)}, s32[16,4]{0,1:T(4,128)S(1)}, f32[16,2,1,16,128]{4,3,0,2,1:T(8,128)S(1)}, s32[]{:T(128)}) %tuple.138), condition=%wide.while_cond, body=%wide.while_body.sunk | while | flops 2 | bytes 32893 | solution.py:67
  248.1 1.9 collective-permute-start
  251.7 3.1 collective-permute-done
  255.6 1.9 collective-permute-start.1
  257.5 2.4 collective-permute-start.2
  260.5 2.3 collective-permute-done.2
  265.2 30.0 %while.28 = (s32[]{:T(128)}, f32[2,1,32,144]{3,2,1,0:T(8,128)S(1)}, s32[16,4]{0,1:T(4,128)S(1)}, f32[16,2,1,16,128]{4,3,0,2,1:T(8,128)S(1)}, s32[]{:T(128)}) while((s32[]{:T(128)}, f32[2,1,32,144]{3,2,1,0:T(8,128)S(1)}, s32[16,4]{0,1:T(4,128)S(1)}, f32[16,2,1,16,128]{4,3,0,2,1:T(8,128)S(1)}, s32[]{:T(128)}) %tuple.138), condition=%wide.while_cond, body=%wide.while_body.sunk | while | flops 2 | bytes 32893 | solution.py:67
  295.2 1.9 collective-permute-start
  298.9 3.1 collective-permute-done
  302.7 1.9 collective-permute-start.1
  304.6 2.4 collective-permute-start.2
  307.6 2.3 collective-permute-done.2
  312.3 30.0 %while.28 = (s32[]{:T(128)}, f32[2,1,32,144]{3,2,1,0:T(8,128)S(1)}, s32[16,4]{0,1:T(4,128)S(1)}, f32[16,2,1,16,128]{4,3,0,2,1:T(8,128)S(1)}, s32[]{:T(128)}) while((s32[]{:T(128)}, f32[2,1,32,144]{3,2,1,0:T(8,128)S(1)}, s32[16,4]{0,1:T(4,128)S(1)}, f32[16,2,1,16,128]{4,3,0,2,1:T(8,128)S(1)}, s32[]{:T(128)}) %tuple.138), condition=%wide.while_cond, body=%wide.while_body.sunk | while | flops 2 | bytes 32893 | solution.py:67
  342.4 1.9 collective-permute-start
  346.0 3.1 collective-permute-done
  349.9 1.9 collective-permute-start.1
  351.8 2.4 collective-permute-start.2
  354.8 2.3 collective-permute-done.2
  359.5 30.0 %while.28 = (s32[]{:T(128)}, f32[2,1,32,144]{3,2,1,0:T(8,128)S(1)}, s32[16,4]{0,1:T(4,128)S(1)}, f32[16,2,1,16,128]{4,3,0,2,1:T(8,128)S(1)}, s32[]{:T(128)}) while((s32[]{:T(128)}, f32[2,1,32,144]{3,2,1,0:T(8,128)S(1)}, s32[16,4]{0,1:T(4,128)S(1)}, f32[16,2,1,16,128]{4,3,0,2,1:T(8,128)S(1)}, s32[]{:T(128)}) %tuple.138), condition=%wide.while_cond, body=%wide.while_body.sunk | while | flops 2 | bytes 32893 | solution.py:67
  389.5 1.9 collective-permute-start
  393.2 3.1 collective-permute-done
  397.0 1.9 collective-permute-start.1
  398.9 2.4 collective-permute-start.2
  401.9 2.3 collective-permute-done.2
  406.6 30.0 %while.28 = (s32[]{:T(128)}, f32[2,1,32,144]{3,2,1,0:T(8,128)S(1)}, s32[16,4]{0,1:T(4,128)S(1)}, f32[16,2,1,16,128]{4,3,0,2,1:T(8,128)S(1)}, s32[]{:T(128)}) while((s32[]{:T(128)}, f32[2,1,32,144]{3,2,1,0:T(8,128)S(1)}, s32[16,4]{0,1:T(4,128)S(1)}, f32[16,2,1,16,128]{4,3,0,2,1:T(8,128)S(1)}, s32[]{:T(128)}) %tuple.138), condition=%wide.while_cond, body=%wide.while_body.sunk | while | flops 2 | bytes 32893 | solution.py:67
  (723 shorter events, 316.4 us)
Async XLA Ops:
  0.8 6.4 %collective-permute-start.3 = (s32[2,12,128]{2,1,0:T(8,128)S(1)}, s32[2,12,128]{2,1,0:T(8,128)S(1)}, u32[]{:S(2)}, u32[]{:S(2)}) collective-permute-start(s32[2,12,128]{2,1,0:T(8,128)S(1)} %get-tuple-element.478), channel_id=1, source_target_pairs={{0,1},{1,2},{2,3},{4,5},{5,6},{6,7},{8,9},{9,10},{10,11},{12,13},{... | collective-permute-start | bytes 36872 | tf_op jit(solution)/shard_map/ppermute | solution.py:23
  2.7 5.1 %collective-permute-start.4 = (s32[2,12,128]{2,1,0:T(8,128)S(1)}, s32[2,12,128]{2,1,0:T(8,128)S(1)}, u32[]{:S(2)}, u32[]{:S(2)}) collective-permute-start(s32[2,12,128]{2,1,0:T(8,128)S(1)} %get-tuple-element.479), channel_id=1, source_target_pairs={{1,0},{2,1},{3,2},{5,4},{6,5},{7,6},{9,8},{10,9},{11,10},{13,12},{... | collective-permute-start | bytes 36872 | tf_op jit(solution)/shard_map/ppermute | solution.py:24
  11.2 0.7 copy-start.1
  11.8 6.7 %collective-permute-start = (f32[2,2,1,16,128]{4,3,1,2,0:T(8,128)S(1)}, f32[2,2,1,16,128]{4,3,1,2,0:T(8,128)S(1)}, u32[]{:S(2)}, u32[]{:S(2)}) collective-permute-start(f32[2,2,1,16,128]{4,3,1,2,0:T(8,128)S(1)} %get-tuple-element.728), channel_id=1, source_target_pairs={{0,4},{4,8},{8,12},{12,16},{16,20},{20,24},{24,28},{1,5},{5,9},{9,... | collective-permute-start | bytes 98312 | tf_op jit(solution)/shard_map/while/body/eval_jaxpr/ppermute | solution.py:32
  19.3 5.0 %collective-permute-start.1 = (f32[2,2,1,16,128]{4,3,1,2,0:T(8,128)S(1)}, f32[2,2,1,16,128]{4,3,1,2,0:T(8,128)S(1)}, u32[]{:S(2)}, u32[]{:S(2)}) collective-permute-start(f32[2,2,1,16,128]{4,3,1,2,0:T(8,128)S(1)} %bitcast_select_fusion.2), channel_id=1, source_target_pairs={{1,0},{2,1},{3,2},{5,4},{6,5},{7,6},{9,8},{10,9},{11,10},{13,12},{... | collective-permute-start | bytes 98312 | tf_op jit(solution)/shard_map/while/body/eval_jaxpr/ppermute | solution.py:24
  21.8 5.3 %collective-permute-start.2 = (f32[2,2,1,16,128]{4,3,1,2,0:T(8,128)S(1)}, f32[2,2,1,16,128]{4,3,1,2,0:T(8,128)}, u32[]{:S(2)}, u32[]{:S(2)}) collective-permute-start(f32[2,2,1,16,128]{4,3,1,2,0:T(8,128)S(1)} %bitcast_select_fusion.2), channel_id=1, source_target_pairs={{0,1},{1,2},{2,3},{4,5},{5,6},{6,7},{8,9},{9,10},{10,11},{12,13},{... | collective-permute-start | bytes 98312 | tf_op jit(solution)/shard_map/while/body/eval_jaxpr/ppermute | solution.py:23
  27.9 0.7 copy-start.3
  28.6 0.7 copy-start.2
  59.5 6.7 %collective-permute-start = (f32[2,2,1,16,128]{4,3,1,2,0:T(8,128)S(1)}, f32[2,2,1,16,128]{4,3,1,2,0:T(8,128)S(1)}, u32[]{:S(2)}, u32[]{:S(2)}) collective-permute-start(f32[2,2,1,16,128]{4,3,1,2,0:T(8,128)S(1)} %get-tuple-element.728), channel_id=1, source_target_pairs={{0,4},{4,8},{8,12},{12,16},{16,20},{20,24},{24,28},{1,5},{5,9},{9,... | collective-permute-start | bytes 98312 | tf_op jit(solution)/shard_map/while/body/eval_jaxpr/ppermute | solution.py:32
  67.0 4.9 %collective-permute-start.1 = (f32[2,2,1,16,128]{4,3,1,2,0:T(8,128)S(1)}, f32[2,2,1,16,128]{4,3,1,2,0:T(8,128)S(1)}, u32[]{:S(2)}, u32[]{:S(2)}) collective-permute-start(f32[2,2,1,16,128]{4,3,1,2,0:T(8,128)S(1)} %bitcast_select_fusion.2), channel_id=1, source_target_pairs={{1,0},{2,1},{3,2},{5,4},{6,5},{7,6},{9,8},{10,9},{11,10},{13,12},{... | collective-permute-start | bytes 98312 | tf_op jit(solution)/shard_map/while/body/eval_jaxpr/ppermute | solution.py:24
  68.9 5.3 %collective-permute-start.2 = (f32[2,2,1,16,128]{4,3,1,2,0:T(8,128)S(1)}, f32[2,2,1,16,128]{4,3,1,2,0:T(8,128)}, u32[]{:S(2)}, u32[]{:S(2)}) collective-permute-start(f32[2,2,1,16,128]{4,3,1,2,0:T(8,128)S(1)} %bitcast_select_fusion.2), channel_id=1, source_target_pairs={{0,1},{1,2},{2,3},{4,5},{5,6},{6,7},{8,9},{9,10},{10,11},{12,13},{... | collective-permute-start | bytes 98312 | tf_op jit(solution)/shard_map/while/body/eval_jaxpr/ppermute | solution.py:23
  75.0 0.7 copy-start.3
  75.8 0.7 copy-start.2
  106.7 6.7 %collective-permute-start = (f32[2,2,1,16,128]{4,3,1,2,0:T(8,128)S(1)}, f32[2,2,1,16,128]{4,3,1,2,0:T(8,128)S(1)}, u32[]{:S(2)}, u32[]{:S(2)}) collective-permute-start(f32[2,2,1,16,128]{4,3,1,2,0:T(8,128)S(1)} %get-tuple-element.728), channel_id=1, source_target_pairs={{0,4},{4,8},{8,12},{12,16},{16,20},{20,24},{24,28},{1,5},{5,9},{9,... | collective-permute-start | bytes 98312 | tf_op jit(solution)/shard_map/while/body/eval_jaxpr/ppermute | solution.py:32
  114.1 4.9 %collective-permute-start.1 = (f32[2,2,1,16,128]{4,3,1,2,0:T(8,128)S(1)}, f32[2,2,1,16,128]{4,3,1,2,0:T(8,128)S(1)}, u32[]{:S(2)}, u32[]{:S(2)}) collective-permute-start(f32[2,2,1,16,128]{4,3,1,2,0:T(8,128)S(1)} %bitcast_select_fusion.2), channel_id=1, source_target_pairs={{1,0},{2,1},{3,2},{5,4},{6,5},{7,6},{9,8},{10,9},{11,10},{13,12},{... | collective-permute-start | bytes 98312 | tf_op jit(solution)/shard_map/while/body/eval_jaxpr/ppermute | solution.py:24
  116.1 5.3 %collective-permute-start.2 = (f32[2,2,1,16,128]{4,3,1,2,0:T(8,128)S(1)}, f32[2,2,1,16,128]{4,3,1,2,0:T(8,128)}, u32[]{:S(2)}, u32[]{:S(2)}) collective-permute-start(f32[2,2,1,16,128]{4,3,1,2,0:T(8,128)S(1)} %bitcast_select_fusion.2), channel_id=1, source_target_pairs={{0,1},{1,2},{2,3},{4,5},{5,6},{6,7},{8,9},{9,10},{10,11},{12,13},{... | collective-permute-start | bytes 98312 | tf_op jit(solution)/shard_map/while/body/eval_jaxpr/ppermute | solution.py:23
  122.2 0.7 copy-start.3
  122.9 0.7 copy-start.2
  153.8 6.7 %collective-permute-start = (f32[2,2,1,16,128]{4,3,1,2,0:T(8,128)S(1)}, f32[2,2,1,16,128]{4,3,1,2,0:T(8,128)S(1)}, u32[]{:S(2)}, u32[]{:S(2)}) collective-permute-start(f32[2,2,1,16,128]{4,3,1,2,0:T(8,128)S(1)} %get-tuple-element.728), channel_id=1, source_target_pairs={{0,4},{4,8},{8,12},{12,16},{16,20},{20,24},{24,28},{1,5},{5,9},{9,... | collective-permute-start | bytes 98312 | tf_op jit(solution)/shard_map/while/body/eval_jaxpr/ppermute | solution.py:32
  161.3 4.9 %collective-permute-start.1 = (f32[2,2,1,16,128]{4,3,1,2,0:T(8,128)S(1)}, f32[2,2,1,16,128]{4,3,1,2,0:T(8,128)S(1)}, u32[]{:S(2)}, u32[]{:S(2)}) collective-permute-start(f32[2,2,1,16,128]{4,3,1,2,0:T(8,128)S(1)} %bitcast_select_fusion.2), channel_id=1, source_target_pairs={{1,0},{2,1},{3,2},{5,4},{6,5},{7,6},{9,8},{10,9},{11,10},{13,12},{... | collective-permute-start | bytes 98312 | tf_op jit(solution)/shard_map/while/body/eval_jaxpr/ppermute | solution.py:24
  163.2 5.3 %collective-permute-start.2 = (f32[2,2,1,16,128]{4,3,1,2,0:T(8,128)S(1)}, f32[2,2,1,16,128]{4,3,1,2,0:T(8,128)}, u32[]{:S(2)}, u32[]{:S(2)}) collective-permute-start(f32[2,2,1,16,128]{4,3,1,2,0:T(8,128)S(1)} %bitcast_select_fusion.2), channel_id=1, source_target_pairs={{0,1},{1,2},{2,3},{4,5},{5,6},{6,7},{8,9},{9,10},{10,11},{12,13},{... | collective-permute-start | bytes 98312 | tf_op jit(solution)/shard_map/while/body/eval_jaxpr/ppermute | solution.py:23
  169.3 0.7 copy-start.3
  170.1 0.7 copy-start.2
  201.0 6.7 %collective-permute-start = (f32[2,2,1,16,128]{4,3,1,2,0:T(8,128)S(1)}, f32[2,2,1,16,128]{4,3,1,2,0:T(8,128)S(1)}, u32[]{:S(2)}, u32[]{:S(2)}) collective-permute-start(f32[2,2,1,16,128]{4,3,1,2,0:T(8,128)S(1)} %get-tuple-element.728), channel_id=1, source_target_pairs={{0,4},{4,8},{8,12},{12,16},{16,20},{20,24},{24,28},{1,5},{5,9},{9,... | collective-permute-start | bytes 98312 | tf_op jit(solution)/shard_map/while/body/eval_jaxpr/ppermute | solution.py:32
  208.4 4.9 %collective-permute-start.1 = (f32[2,2,1,16,128]{4,3,1,2,0:T(8,128)S(1)}, f32[2,2,1,16,128]{4,3,1,2,0:T(8,128)S(1)}, u32[]{:S(2)}, u32[]{:S(2)}) collective-permute-start(f32[2,2,1,16,128]{4,3,1,2,0:T(8,128)S(1)} %bitcast_select_fusion.2), channel_id=1, source_target_pairs={{1,0},{2,1},{3,2},{5,4},{6,5},{7,6},{9,8},{10,9},{11,10},{13,12},{... | collective-permute-start | bytes 98312 | tf_op jit(solution)/shard_map/while/body/eval_jaxpr/ppermute | solution.py:24
  210.3 5.3 %collective-permute-start.2 = (f32[2,2,1,16,128]{4,3,1,2,0:T(8,128)S(1)}, f32[2,2,1,16,128]{4,3,1,2,0:T(8,128)}, u32[]{:S(2)}, u32[]{:S(2)}) collective-permute-start(f32[2,2,1,16,128]{4,3,1,2,0:T(8,128)S(1)} %bitcast_select_fusion.2), channel_id=1, source_target_pairs={{0,1},{1,2},{2,3},{4,5},{5,6},{6,7},{8,9},{9,10},{10,11},{12,13},{... | collective-permute-start | bytes 98312 | tf_op jit(solution)/shard_map/while/body/eval_jaxpr/ppermute | solution.py:23
  216.5 0.7 copy-start.3
  217.2 0.7 copy-start.2
  248.1 6.7 %collective-permute-start = (f32[2,2,1,16,128]{4,3,1,2,0:T(8,128)S(1)}, f32[2,2,1,16,128]{4,3,1,2,0:T(8,128)S(1)}, u32[]{:S(2)}, u32[]{:S(2)}) collective-permute-start(f32[2,2,1,16,128]{4,3,1,2,0:T(8,128)S(1)} %get-tuple-element.728), channel_id=1, source_target_pairs={{0,4},{4,8},{8,12},{12,16},{16,20},{20,24},{24,28},{1,5},{5,9},{9,... | collective-permute-start | bytes 98312 | tf_op jit(solution)/shard_map/while/body/eval_jaxpr/ppermute | solution.py:32
  255.6 4.9 %collective-permute-start.1 = (f32[2,2,1,16,128]{4,3,1,2,0:T(8,128)S(1)}, f32[2,2,1,16,128]{4,3,1,2,0:T(8,128)S(1)}, u32[]{:S(2)}, u32[]{:S(2)}) collective-permute-start(f32[2,2,1,16,128]{4,3,1,2,0:T(8,128)S(1)} %bitcast_select_fusion.2), channel_id=1, source_target_pairs={{1,0},{2,1},{3,2},{5,4},{6,5},{7,6},{9,8},{10,9},{11,10},{13,12},{... | collective-permute-start | bytes 98312 | tf_op jit(solution)/shard_map/while/body/eval_jaxpr/ppermute | solution.py:24
  257.5 5.3 %collective-permute-start.2 = (f32[2,2,1,16,128]{4,3,1,2,0:T(8,128)S(1)}, f32[2,2,1,16,128]{4,3,1,2,0:T(8,128)}, u32[]{:S(2)}, u32[]{:S(2)}) collective-permute-start(f32[2,2,1,16,128]{4,3,1,2,0:T(8,128)S(1)} %bitcast_select_fusion.2), channel_id=1, source_target_pairs={{0,1},{1,2},{2,3},{4,5},{5,6},{6,7},{8,9},{9,10},{10,11},{12,13},{... | collective-permute-start | bytes 98312 | tf_op jit(solution)/shard_map/while/body/eval_jaxpr/ppermute | solution.py:23
  263.6 0.7 copy-start.3
  264.3 0.7 copy-start.2
  295.2 6.7 %collective-permute-start = (f32[2,2,1,16,128]{4,3,1,2,0:T(8,128)S(1)}, f32[2,2,1,16,128]{4,3,1,2,0:T(8,128)S(1)}, u32[]{:S(2)}, u32[]{:S(2)}) collective-permute-start(f32[2,2,1,16,128]{4,3,1,2,0:T(8,128)S(1)} %get-tuple-element.728), channel_id=1, source_target_pairs={{0,4},{4,8},{8,12},{12,16},{16,20},{20,24},{24,28},{1,5},{5,9},{9,... | collective-permute-start | bytes 98312 | tf_op jit(solution)/shard_map/while/body/eval_jaxpr/ppermute | solution.py:32
  302.7 4.9 %collective-permute-start.1 = (f32[2,2,1,16,128]{4,3,1,2,0:T(8,128)S(1)}, f32[2,2,1,16,128]{4,3,1,2,0:T(8,128)S(1)}, u32[]{:S(2)}, u32[]{:S(2)}) collective-permute-start(f32[2,2,1,16,128]{4,3,1,2,0:T(8,128)S(1)} %bitcast_select_fusion.2), channel_id=1, source_target_pairs={{1,0},{2,1},{3,2},{5,4},{6,5},{7,6},{9,8},{10,9},{11,10},{13,12},{... | collective-permute-start | bytes 98312 | tf_op jit(solution)/shard_map/while/body/eval_jaxpr/ppermute | solution.py:24
  304.6 5.3 %collective-permute-start.2 = (f32[2,2,1,16,128]{4,3,1,2,0:T(8,128)S(1)}, f32[2,2,1,16,128]{4,3,1,2,0:T(8,128)}, u32[]{:S(2)}, u32[]{:S(2)}) collective-permute-start(f32[2,2,1,16,128]{4,3,1,2,0:T(8,128)S(1)} %bitcast_select_fusion.2), channel_id=1, source_target_pairs={{0,1},{1,2},{2,3},{4,5},{5,6},{6,7},{8,9},{9,10},{10,11},{12,13},{... | collective-permute-start | bytes 98312 | tf_op jit(solution)/shard_map/while/body/eval_jaxpr/ppermute | solution.py:23
  310.7 0.7 copy-start.3
  311.5 0.7 copy-start.2
  342.4 6.7 %collective-permute-start = (f32[2,2,1,16,128]{4,3,1,2,0:T(8,128)S(1)}, f32[2,2,1,16,128]{4,3,1,2,0:T(8,128)S(1)}, u32[]{:S(2)}, u32[]{:S(2)}) collective-permute-start(f32[2,2,1,16,128]{4,3,1,2,0:T(8,128)S(1)} %get-tuple-element.728), channel_id=1, source_target_pairs={{0,4},{4,8},{8,12},{12,16},{16,20},{20,24},{24,28},{1,5},{5,9},{9,... | collective-permute-start | bytes 98312 | tf_op jit(solution)/shard_map/while/body/eval_jaxpr/ppermute | solution.py:32
  349.9 4.9 %collective-permute-start.1 = (f32[2,2,1,16,128]{4,3,1,2,0:T(8,128)S(1)}, f32[2,2,1,16,128]{4,3,1,2,0:T(8,128)S(1)}, u32[]{:S(2)}, u32[]{:S(2)}) collective-permute-start(f32[2,2,1,16,128]{4,3,1,2,0:T(8,128)S(1)} %bitcast_select_fusion.2), channel_id=1, source_target_pairs={{1,0},{2,1},{3,2},{5,4},{6,5},{7,6},{9,8},{10,9},{11,10},{13,12},{... | collective-permute-start | bytes 98312 | tf_op jit(solution)/shard_map/while/body/eval_jaxpr/ppermute | solution.py:24
  351.8 5.3 %collective-permute-start.2 = (f32[2,2,1,16,128]{4,3,1,2,0:T(8,128)S(1)}, f32[2,2,1,16,128]{4,3,1,2,0:T(8,128)}, u32[]{:S(2)}, u32[]{:S(2)}) collective-permute-start(f32[2,2,1,16,128]{4,3,1,2,0:T(8,128)S(1)} %bitcast_select_fusion.2), channel_id=1, source_target_pairs={{0,1},{1,2},{2,3},{4,5},{5,6},{6,7},{8,9},{9,10},{10,11},{12,13},{... | collective-permute-start | bytes 98312 | tf_op jit(solution)/shard_map/while/body/eval_jaxpr/ppermute | solution.py:23
  357.9 0.7 copy-start.3
  358.6 0.7 copy-start.2
  389.5 6.7 %collective-permute-start = (f32[2,2,1,16,128]{4,3,1,2,0:T(8,128)S(1)}, f32[2,2,1,16,128]{4,3,1,2,0:T(8,128)S(1)}, u32[]{:S(2)}, u32[]{:S(2)}) collective-permute-start(f32[2,2,1,16,128]{4,3,1,2,0:T(8,128)S(1)} %get-tuple-element.728), channel_id=1, source_target_pairs={{0,4},{4,8},{8,12},{12,16},{16,20},{20,24},{24,28},{1,5},{5,9},{9,... | collective-permute-start | bytes 98312 | tf_op jit(solution)/shard_map/while/body/eval_jaxpr/ppermute | solution.py:32
  397.0 4.9 %collective-permute-start.1 = (f32[2,2,1,16,128]{4,3,1,2,0:T(8,128)S(1)}, f32[2,2,1,16,128]{4,3,1,2,0:T(8,128)S(1)}, u32[]{:S(2)}, u32[]{:S(2)}) collective-permute-start(f32[2,2,1,16,128]{4,3,1,2,0:T(8,128)S(1)} %bitcast_select_fusion.2), channel_id=1, source_target_pairs={{1,0},{2,1},{3,2},{5,4},{6,5},{7,6},{9,8},{10,9},{11,10},{13,12},{... | collective-permute-start | bytes 98312 | tf_op jit(solution)/shard_map/while/body/eval_jaxpr/ppermute | solution.py:24
  398.9 5.3 %collective-permute-start.2 = (f32[2,2,1,16,128]{4,3,1,2,0:T(8,128)S(1)}, f32[2,2,1,16,128]{4,3,1,2,0:T(8,128)}, u32[]{:S(2)}, u32[]{:S(2)}) collective-permute-start(f32[2,2,1,16,128]{4,3,1,2,0:T(8,128)S(1)} %bitcast_select_fusion.2), channel_id=1, source_target_pairs={{0,1},{1,2},{2,3},{4,5},{5,6},{6,7},{8,9},{9,10},{10,11},{12,13},{... | collective-permute-start | bytes 98312 | tf_op jit(solution)/shard_map/while/body/eval_jaxpr/ppermute | solution.py:23
  405.0 0.7 copy-start.3
  405.8 0.7 copy-start.2
  436.7 0.7 copy-start
where the time goes:
time: 445 us; the launch traced here: 437 us
  local copies, waits for them, and re-layouts  282 us (63%)
  starting transfers between devices  63.8 us (14%)
  waiting for transfers between devices  47.4 us (11%)
  other arithmetic  41 us (9%)
    gather x432, local copies, waits for them, and re-layouts  269 us
    ppermute x9, waiting for transfers between devices, shifted_2(): return lax.ppermute(block, axis, route)  25.4 us
    ppermute x10, starting transfers between devices, with_halo(): before = lax.ppermute(last, axis, up)  23.1 us
    ppermute x10, waiting for transfers between devices, with_halo(): before = lax.ppermute(last, axis, up)  21.4 us
    ppermute x10, starting transfers between devices, with_halo(): after = lax.ppermute(leading, axis, down)  21.4 us
    ppermute x9, starting transfers between devices, shifted_2(): return lax.ppermute(block, axis, route)  19.4 us
    convert_element_type x18, other arithmetic, within_mesh(): return ((row_ids >= 0) & (row_ids < grid_rows)).astype(jnp.float32)[:, None]  10.6 us
  transfers between devices with their start and end apart: 29, of which 19 were waited for; matrix products, arithmetic and copies ran while one was open for 5% of the time, Pallas kernels for 0%

commit v1 on v0

v1 whole, which is shorter than its diff:
```python
import functools

import jax
import jax.numpy as jnp
from jax import lax
from jax.experimental import pallas as pl
from jax.experimental.pallas import tpu as pltpu
from jax.sharding import PartitionSpec as P

OFF_Y = 8
OFF_X = 8
TAP_ROWS = (0, -4, -3, -2, -1, 1, 2, 3, 4, 0, 0, 0, 0)
TAP_COLS = (0, 0, 0, 0, 0, 0, 0, 0, 0, -2, -1, 1, 2)
PAD = 8
SUB = 8


def swap(block, axis, bit):
    count = lax.axis_size(axis)
    return lax.ppermute(block, axis, [(i, i ^ bit) for i in range(count)])


def bits_of(count):
    return [1 << k for k in reversed(range(count.bit_length() - 1))]


def reversed_bits(value, count):
    width = count.bit_length() - 1
    total = 0
    for k in range(width):
        total = total + (((value >> k) & 1) << (width - 1 - k))
    return total


def image_kernel(
    sizes, offsets, table, surf_own, surf_other, bins_own, bins_other, image, wide, first, second
):
    depth_count, line_count, levels, row_count, freq_count, row_chunk = sizes
    depth_index = lax.axis_index("depth")
    line_index = lax.axis_index("xline")
    width = image.shape[3]
    grid_rows = row_count * line_count
    taps = len(TAP_ROWS)
    near_count = line_count // 2

    for row in range(table.shape[0]):
        wide[row] = jnp.broadcast_to(table[row : row + 1, :], (SUB, width))

    zeros = jnp.zeros((PAD, width), jnp.float32)
    for array in range(4 * freq_count):
        for buffer in (first, second):
            buffer[array, 0:PAD, :] = zeros
            buffer[array, PAD + grid_rows : 2 * PAD + grid_rows, :] = zeros

    for slot in range(near_count):
        for own, source in ((0, surf_own), (1, surf_other)):
            line = line_index ^ (2 * reversed_bits(slot, near_count) + own)
            start = pl.multiple_of(PAD + line * row_count, SUB)
            for array in range(4 * freq_count):
                block = source[slot, array]
                if array >= 3 * freq_count:
                    block = -block
                first[array, pl.ds(start, row_count), :] = block

    lane = lax.broadcasted_iota(jnp.int32, (SUB, width), 1)
    inside = {
        step: (lane + step >= 0) & (lane + step < width) for step in sorted(set(TAP_COLS) - {0})
    }

    def level(slab_slot, level_index, source, target):
        def chunk_step(chunk, carry):
            for block in range(row_chunk // SUB):
                row = pl.multiple_of(chunk * row_chunk + block * SUB, SUB)
                line = (row // row_count) ^ line_index
                slot = reversed_bits(line // 2, near_count)
                inner = pl.multiple_of(row % row_count, SUB)
                own = bins_own[slot, slab_slot, level_index, pl.ds(inner, SUB), :]
                other = bins_other[slot, slab_slot, level_index, pl.ds(inner, SUB), :]
                bins = jnp.where((line & 1) == 0, own, other)
                for freq in range(freq_count):
                    sums = [None] * 4
                    centre = None
                    for tap in range(taps):
                        coefs = [
                            jnp.take_along_axis(
                                wide[(tap * 2 + part) * freq_count + freq],
                                bins,
                                axis=1,
                                mode="promise_in_bounds",
                            )
                            for part in range(2)
                        ]
                        step = TAP_COLS[tap]
                        if step == 0:
                            fields = [
                                source[
                                    array * freq_count + freq,
                                    pl.ds(PAD + row + TAP_ROWS[tap], SUB),
                                    :,
                                ]
                                for array in range(4)
                            ]
                            if tap == 0:
                                centre = fields
                        else:
                            fields = [
                                jnp.where(
                                    inside[step], pltpu.roll(value, (-step) % width, 1), 0.0
                                )
                                for value in centre
                            ]
                        for field in range(2):
                            real, imag = fields[2 * field], fields[2 * field + 1]
                            term_real = coefs[0] * real - coefs[1] * imag
                            term_imag = coefs[0] * imag + coefs[1] * real
                            for part, term in ((0, term_real), (1, term_imag)):
                                place = 2 * field + part
                                sums[place] = term if sums[place] is None else sums[place] + term
                    for array in range(4):
                        target[array * freq_count + freq, pl.ds(PAD + row, SUB), :] = sums[array]
            return carry

        lax.fori_loop(0, grid_rows // row_chunk, chunk_step, 0)

    def slab_step(slab, carry):
        slot = reversed_bits(slab ^ depth_index, depth_count)
        buffers = (first, second)
        for level_index in range(levels):
            level(slot, level_index, buffers[level_index % 2], buffers[1 - level_index % 2])
        if levels % 2:
            first[...] = second[...]
        return carry

    lax.fori_loop(0, depth_index + 1, slab_step, 0)

    base = pl.multiple_of(PAD + line_index * row_count, SUB)
    lanes = lax.broadcasted_iota(jnp.int32, (row_count, width), 1)
    sources = [first[array, pl.ds(base, row_count), :] for array in range(2 * freq_count)]

    for h in range(image.shape[1]):
        dy = offsets[h, 0]
        dx = offsets[h, 1]
        valid = (lanes + dx >= 0) & (lanes + dx < width)
        total = None
        for array in range(2 * freq_count):
            value = first[2 * freq_count + array, pl.ds(base + dy, row_count), :]
            term = sources[array] * pltpu.roll(value, lax.rem(width - dx, width), 1)
            if array >= freq_count:
                term = -term
            total = term if total is None else total + term
        image[0, h] = jnp.where(valid, total, 0.0)


def shards(surface_fields, stencil_table, velocity_bins, offset_list):
    depth_count = lax.axis_size("depth")
    line_count = lax.axis_size("xline")
    row_count = surface_fields.shape[3]
    width = surface_fields.shape[4]
    freq_count = surface_fields.shape[2]
    levels = velocity_bins.shape[1]
    grid_rows = row_count * line_count
    row_chunk = next(rows for rows in (64, 32, 16, 8) if grid_rows % rows == 0)

    surf = surface_fields.reshape(1, 4 * freq_count, row_count, width)
    bins = velocity_bins
    line_bits = bits_of(line_count)[:-1]
    for bit in line_bits:
        surf = jnp.concatenate([surf, swap(surf, "xline", bit)], axis=0)
    for bit in bits_of(depth_count):
        bins = jnp.concatenate([bins, swap(bins, "depth", bit)], axis=0)
    bins = bins[None]
    for bit in line_bits:
        bins = jnp.concatenate([bins, swap(bins, "xline", bit)], axis=0)
    surf_other = swap(surf, "xline", 1)
    bins_other = swap(bins, "xline", 1)

    table = stencil_table.reshape(-1, stencil_table.shape[3])
    sizes = (depth_count, line_count, levels, row_count, freq_count, row_chunk)
    field_shape = (4 * freq_count, grid_rows + 2 * PAD, width)
    whole = pl.BlockSpec(memory_space=pltpu.VMEM)
    return pl.pallas_call(
        functools.partial(image_kernel, sizes),
        out_shape=jax.ShapeDtypeStruct((1, offset_list.shape[0], row_count, width), jnp.float32),
        in_specs=[pl.BlockSpec(memory_space=pltpu.SMEM)] + [whole] * 5,
        out_specs=whole,
        scratch_shapes=[
            pltpu.VMEM((table.shape[0], SUB, width), jnp.float32),
            pltpu.VMEM(field_shape, jnp.float32),
            pltpu.VMEM(field_shape, jnp.float32),
        ],
        name="continuation",
    )(offset_list, table, surf, surf_other, bins, bins_other)


def solution(mesh):
    return jax.shard_map(
        shards,
        mesh=mesh,
        in_specs=(P(None, None, None, "xline", None), P(), P("depth", None, "xline", None), P()),
        out_specs=P("depth", None, "xline", None),
        check_vma=False,
    )
```

time: 445 us -> 38.9 us (0.09)
  the two profiles are of different devices: /device:TPU:26 before, /device:TPU:29 now
where the time goes in v1:
time: 38.9 us; the launch traced here: 38.7 us
  Pallas kernels  15.5 us (40%)
  waiting for transfers between devices  11.6 us (30%)
  starting transfers between devices  8.07 us (21%)
  local copies, waits for them, and re-layouts  2.66 us (7%)
  other arithmetic  0.76 us (2%)
    pallas_call x1, Pallas kernels, shards(): pl.pallas_call(functools.partial(image_kernel, sizes), out_shape=jax.Shap...  15.5 us
    ppermute x7, waiting for transfers between devices, swap(): return lax.ppermute(block, axis, [(i, i ^ bit) for i in range(count)])  11.6 us
    ppermute x7, starting transfers between devices, swap(): return lax.ppermute(block, axis, [(i, i ^ bit) for i in range(count)])  8.07 us
    unnamed x17, local copies, waits for them, and re-layouts  2.04 us
  transfers between devices with their start and end apart: 7, of which 4 were waited for; matrix products, arithmetic and copies ran while one was open for 3% of the time, Pallas kernels for 0%

profile of v1, /device:TPU:29, one launch (start us, length us, event | category | flops | bytes accessed | tf_op | source)
XLA Modules:
  0.0 38.7 jit_solution(3604658697773377019)
XLA Ops:
  0.0 0.0 copy-start.3
  0.0 0.1 collective-permute-start.2
  0.1 3.7 %collective-permute-done.2 = s32[1,2,16,128]{3,2,1,0:T(8,128)S(1)} collective-permute-done((s32[1,2,16,128]{3,2,1,0:T(8,128)}, s32[1,2,16,128]{3,2,1,0:T(8,128)S(1)}, u32[]{:S(2)}, u32[]{:S(2)}) %collective-permute-start.2) | collective-permute-done | bytes 16416 | tf_op jit(solution)/shard_map/ppermute | solution.py:20
  3.8 0.7 %pad_add_fusion.2 = s32[2,2,16,128]{3,2,1,0:T(8,128)S(1)} fusion(s32[1,2,16,128]{3,2,1,0:T(8,128)S(1)} %collective-permute-done.2, s32[1,2,16,128]{3,2,1,0:T(8,128)} %param.6), kind=kLoop, calls=%fused_computation.4 | loop fusion | flops 8192 | bytes 65536 | tf_op jit(solution)/shard_map/concatenate | solution.py:170
  4.5 0.1 collective-permute-start.3
  4.6 2.7 %collective-permute-done.3 = s32[2,2,16,128]{3,2,1,0:T(8,128)S(1)} collective-permute-done((s32[2,2,16,128]{3,2,1,0:T(8,128)S(1)}, s32[2,2,16,128]{3,2,1,0:T(8,128)S(1)}, u32[]{:S(2)}, u32[]{:S(2)}) %collective-permute-start.3) | collective-permute-done | bytes 32800 | tf_op jit(solution)/shard_map/ppermute | solution.py:20
  7.3 0.0 copy-done.3
  7.3 0.0 copy-start.5
  7.3 0.3 collective-permute-start.4
  7.6 2.9 %collective-permute-done.4 = s32[4,2,16,128]{3,2,1,0:T(8,128)S(1)} collective-permute-done((s32[4,2,16,128]{3,2,1,0:T(8,128)S(1)}, s32[4,2,16,128]{3,2,1,0:T(8,128)S(1)}, u32[]{:S(2)}, u32[]{:S(2)}) %collective-permute-start.4) | collective-permute-done | bytes 65568 | tf_op jit(solution)/shard_map/ppermute | solution.py:20
  10.5 1.3 %collective-permute-start.5 = (s32[1,8,2,16,128]{4,3,2,1,0:T(8,128)S(1)}, s32[1,8,2,16,128]{4,3,2,1,0:T(8,128)S(1)}, u32[]{:S(2)}, u32[]{:S(2)}) collective-permute-start(s32[1,8,2,16,128]{4,3,2,1,0:T(8,128)S(1)} %add_bitcast_fusion), channel_id=1, source_target_pairs={{0,2},{1,3},{2,0},{3,1},{4,6},{5,7},{6,4},{7,5},{8,10},{9,11},{10,... | collective-permute-start | bytes 393224 | tf_op jit(solution)/shard_map/ppermute | solution.py:20
  11.7 0.0 copy-done.5
  11.7 0.3 collective-permute-start
  12.0 2.3 %collective-permute-done.5 = s32[1,8,2,16,128]{4,3,2,1,0:T(8,128)S(1)} collective-permute-done((s32[1,8,2,16,128]{4,3,2,1,0:T(8,128)S(1)}, s32[1,8,2,16,128]{4,3,2,1,0:T(8,128)S(1)}, u32[]{:S(2)}, u32[]{:S(2)}) %collective-permute-start.5) | collective-permute-done | bytes 131104 | tf_op jit(solution)/shard_map/ppermute | solution.py:20
  14.4 0.0 copy-start
  14.4 0.0 copy-start.7
  14.4 5.3 %collective-permute-start.6 = (s32[2,8,2,16,128]{4,3,2,1,0:T(8,128)S(1)}, s32[2,8,2,16,128]{4,3,2,1,0:T(8,128)S(1)}, u32[]{:S(2)}, u32[]{:S(2)}) collective-permute-start(s32[2,8,2,16,128]{4,3,2,1,0:T(8,128)S(1)} %pad_add_fusion.bins_own), channel_id=1, source_target_pairs={{0,1},{1,0},{2,3},{3,2},{4,5},{5,4},{6,7},{7,6},{8,9},{9,8},{10,11... | collective-permute-start | bytes 786440 | tf_op jit(solution)/shard_map/ppermute | solution.py:20
  19.7 0.0 collective-permute-done
  19.7 0.0 copy-start.6
  19.8 0.0 copy-start.1
  19.8 0.7 %collective-permute-start.1 = (f32[2,8,16,128]{3,2,1,0:T(8,128)S(1)}, f32[2,8,16,128]{3,2,1,0:T(8,128)S(1)}, u32[]{:S(2)}, u32[]{:S(2)}) collective-permute-start(f32[2,8,16,128]{3,2,1,0:T(8,128)S(1)} %pad_maximum_fusion.surf_own), channel_id=1, source_target_pairs={{0,1},{1,0},{2,3},{3,2},{4,5},{5,4},{6,7},{7,6},{8,9},{9,8},{10,11... | collective-permute-start | bytes 393224 | tf_op jit(solution)/shard_map/ppermute | solution.py:20
  20.5 0.0 copy-done.7
  20.5 0.7 %copy.5.offsets = s32[16,2]{1,0:T(8,128)} copy(s32[16,2]{0,1:T(2,128)S(1)} %copy-done.7) | data formatting | bytes 256 | tf_op args[3]
  21.2 0.0 copy-done.6
  21.2 0.6 %reshape.6.table = f32[52,128]{1,0:T(8,128)} reshape(f32[13,2,2,128]{3,2,1,0:T(2,128)S(1)} %copy-done.6) | data formatting | bytes 53248 | tf_op jit(solution)/shard_map/reshape | solution.py:177
  21.8 0.0 collective-permute-done.1.surf_other
  21.8 0.0 copy-start.4
  21.8 0.0 collective-permute-done.6.bins_other
  21.8 0.0 copy-done
  21.8 0.0 copy-done.1
  21.8 0.6 %copy-done.4 = f32[2,8,16,128]{3,2,1,0:T(8,128)} copy-done((f32[2,8,16,128]{3,2,1,0:T(8,128)}, f32[2,8,16,128]{3,2,1,0:T(8,128)S(1)}, u32[]{:S(2)}) %copy-start.4) | copy-done | bytes 131096
  22.5 0.0 copy-start.2
  22.5 0.7 %copy-done.2 = s32[2,8,2,16,128]{4,3,2,1,0:T(8,128)} copy-done((s32[2,8,2,16,128]{4,3,2,1,0:T(8,128)}, s32[2,8,2,16,128]{4,3,2,1,0:T(8,128)S(1)}, u32[]{:S(2)}) %copy-start.2) | copy-done | bytes 262168
  23.2 15.5 %continuation.1 = f32[1,16,16,128]{3,2,1,0:T(8,128)} custom-call(s32[16,2]{1,0:T(8,128)} %copy.5.offsets, f32[52,128]{1,0:T(8,128)} %reshape.6.table, f32[2,8,16,128]{3,2,1,0:T(8,128)} %copy-done.1, f32[2,8,16,128]{3,2,1,0:T(8,128)} %copy-done.4, s32[2,8,2,16,128]{4,3,2,1,0:T(8,128)} %copy-done, s32[2,8,2,16,128]{4,3,2,1,0:T(8,128)} %copy-done.2), custom_call_target="tpu_custom_call" | custom-call | tf_op jit(solution)/shard_map/continuation/pallas_call | solution.py:181
  (4 shorter events, 0.0 us)
Async XLA Ops:
  0.0 7.3 %copy-start.3 = (s32[1,2,16,128]{3,2,1,0:T(8,128)S(1)}, s32[1,2,16,128]{3,2,1,0:T(8,128)}, u32[]{:S(2)}) copy-start(s32[1,2,16,128]{3,2,1,0:T(8,128)} %param.6) | copy-start | bytes 49156
  0.0 3.8 %collective-permute-start.2 = (s32[1,2,16,128]{3,2,1,0:T(8,128)}, s32[1,2,16,128]{3,2,1,0:T(8,128)S(1)}, u32[]{:S(2)}, u32[]{:S(2)}) collective-permute-start(s32[1,2,16,128]{3,2,1,0:T(8,128)} %param.6), channel_id=1, source_target_pairs={{0,16},{4,20},{8,24},{12,28},{16,0},{20,4},{24,8},{28,12},{1,17},{... | collective-permute-start | bytes 49160 | tf_op jit(solution)/shard_map/ppermute | solution.py:20
  4.5 2.8 %collective-permute-start.3 = (s32[2,2,16,128]{3,2,1,0:T(8,128)S(1)}, s32[2,2,16,128]{3,2,1,0:T(8,128)S(1)}, u32[]{:S(2)}, u32[]{:S(2)}) collective-permute-start(s32[2,2,16,128]{3,2,1,0:T(8,128)S(1)} %pad_add_fusion.2), channel_id=1, source_target_pairs={{0,8},{4,12},{8,0},{12,4},{16,24},{20,28},{24,16},{28,20},{1,9},{5... | collective-permute-start | bytes 98312 | tf_op jit(solution)/shard_map/ppermute | solution.py:20
  7.3 4.5 %copy-start.5 = (f32[2,2,2,16,128]{4,3,2,1,0:T(8,128)S(1)}, f32[2,2,2,16,128]{4,3,2,1,0:T(8,128)}, u32[]{:S(2)}) copy-start(f32[2,2,2,16,128]{4,3,2,1,0:T(8,128)} %param.4) | copy-start | bytes 196612
  7.3 3.2 %collective-permute-start.4 = (s32[4,2,16,128]{3,2,1,0:T(8,128)S(1)}, s32[4,2,16,128]{3,2,1,0:T(8,128)S(1)}, u32[]{:S(2)}, u32[]{:S(2)}) collective-permute-start(s32[4,2,16,128]{3,2,1,0:T(8,128)S(1)} %pad_add_fusion.1), channel_id=1, source_target_pairs={{0,4},{4,0},{8,12},{12,8},{16,20},{20,16},{24,28},{28,24},{1,5},{5... | collective-permute-start | bytes 196616 | tf_op jit(solution)/shard_map/ppermute | solution.py:20
  10.5 3.9 %collective-permute-start.5 = (s32[1,8,2,16,128]{4,3,2,1,0:T(8,128)S(1)}, s32[1,8,2,16,128]{4,3,2,1,0:T(8,128)S(1)}, u32[]{:S(2)}, u32[]{:S(2)}) collective-permute-start(s32[1,8,2,16,128]{4,3,2,1,0:T(8,128)S(1)} %add_bitcast_fusion), channel_id=1, source_target_pairs={{0,2},{1,3},{2,0},{3,1},{4,6},{5,7},{6,4},{7,5},{8,10},{9,11},{10,... | collective-permute-start | bytes 393224 | tf_op jit(solution)/shard_map/ppermute | solution.py:20
  11.7 8.0 %collective-permute-start = (f32[1,8,16,128]{3,2,1,0:T(8,128)S(1)}, f32[1,8,16,128]{3,2,1,0:T(8,128)S(1)}, u32[]{:S(2)}, u32[]{:S(2)}) collective-permute-start(f32[1,8,16,128]{3,2,1,0:T(8,128)S(1)} %bitcast.3), channel_id=1, source_target_pairs={{0,2},{1,3},{2,0},{3,1},{4,6},{5,7},{6,4},{7,5},{8,10},{9,11},{10,... | collective-permute-start | bytes 196616 | tf_op jit(solution)/shard_map/ppermute | solution.py:20
  14.4 7.5 %copy-start = (s32[2,8,2,16,128]{4,3,2,1,0:T(8,128)}, s32[2,8,2,16,128]{4,3,2,1,0:T(8,128)S(1)}, u32[]{:S(2)}) copy-start(s32[2,8,2,16,128]{4,3,2,1,0:T(8,128)S(1)} %pad_add_fusion.bins_own) | copy-start | bytes 786436
  14.4 6.1 %copy-start.7 = (s32[16,2]{0,1:T(2,128)S(1)}, s32[16,2]{0,1:T(2,128)}, u32[]{:S(2)}) copy-start(s32[16,2]{0,1:T(2,128)} %param.7) | copy-start | bytes 388
  14.4 7.4 %collective-permute-start.6 = (s32[2,8,2,16,128]{4,3,2,1,0:T(8,128)S(1)}, s32[2,8,2,16,128]{4,3,2,1,0:T(8,128)S(1)}, u32[]{:S(2)}, u32[]{:S(2)}) collective-permute-start(s32[2,8,2,16,128]{4,3,2,1,0:T(8,128)S(1)} %pad_add_fusion.bins_own), channel_id=1, source_target_pairs={{0,1},{1,0},{2,3},{3,2},{4,5},{5,4},{6,7},{7,6},{8,9},{9,8},{10,11... | collective-permute-start | bytes 786440 | tf_op jit(solution)/shard_map/ppermute | solution.py:20
  19.7 1.5 %copy-start.6 = (f32[13,2,2,128]{3,2,1,0:T(2,128)S(1)}, f32[13,2,2,128]{3,2,1,0:T(2,128)}, u32[]{:S(2)}) copy-start(f32[13,2,2,128]{3,2,1,0:T(2,128)} %param.5) | copy-start | bytes 79876
  19.8 2.1 %copy-start.1 = (f32[2,8,16,128]{3,2,1,0:T(8,128)}, f32[2,8,16,128]{3,2,1,0:T(8,128)S(1)}, u32[]{:S(2)}) copy-start(f32[2,8,16,128]{3,2,1,0:T(8,128)S(1)} %pad_maximum_fusion.surf_own) | copy-start | bytes 393220
  19.8 2.1 %collective-permute-start.1 = (f32[2,8,16,128]{3,2,1,0:T(8,128)S(1)}, f32[2,8,16,128]{3,2,1,0:T(8,128)S(1)}, u32[]{:S(2)}, u32[]{:S(2)}) collective-permute-start(f32[2,8,16,128]{3,2,1,0:T(8,128)S(1)} %pad_maximum_fusion.surf_own), channel_id=1, source_target_pairs={{0,1},{1,0},{2,3},{3,2},{4,5},{5,4},{6,7},{7,6},{8,9},{9,8},{10,11... | collective-permute-start | bytes 393224 | tf_op jit(solution)/shard_map/ppermute | solution.py:20
  21.8 0.7 %copy-start.4 = (f32[2,8,16,128]{3,2,1,0:T(8,128)}, f32[2,8,16,128]{3,2,1,0:T(8,128)S(1)}, u32[]{:S(2)}) copy-start(f32[2,8,16,128]{3,2,1,0:T(8,128)S(1)} %collective-permute-done.1.surf_other) | copy-start | bytes 393220
  22.5 0.7 %copy-start.2 = (s32[2,8,2,16,128]{4,3,2,1,0:T(8,128)}, s32[2,8,2,16,128]{4,3,2,1,0:T(8,128)S(1)}, u32[]{:S(2)}) copy-start(s32[2,8,2,16,128]{4,3,2,1,0:T(8,128)S(1)} %collective-permute-done.6.bins_other) | copy-start | bytes 786436

commit v2 on v1

--- a/solution.py
+++ b/solution.py
@@ -32,22 +32,26 @@
     return total
 
 
-def image_kernel(
-    sizes, offsets, table, surf_own, surf_other, bins_own, bins_other, image, wide, first, second
+def continuation_kernel(
+    sizes, table, surf_own, surf_other, bins_own, bins_other, mine, theirs, wide, first, second
 ):
-    depth_count, line_count, levels, row_count, freq_count, row_chunk = sizes
+    depth_count, line_count, levels, row_count, freqs, row_chunk = sizes
     depth_index = lax.axis_index("depth")
     line_index = lax.axis_index("xline")
-    width = image.shape[3]
+    parity = line_index & 1
+    width = mine.shape[1]
     grid_rows = row_count * line_count
     taps = len(TAP_ROWS)
     near_count = line_count // 2
 
-    for row in range(table.shape[0]):
-        wide[row] = jnp.broadcast_to(table[row : row + 1, :], (SUB, width))
+    for tap in range(taps):
+        for part in range(2):
+            for freq in range(freqs):
+                row = table[tap, part, pl.ds(parity * freqs + freq, 1), :]
+                wide[(tap * 2 + part) * freqs + freq] = jnp.broadcast_to(row, (SUB, width))
 
     zeros = jnp.zeros((PAD, width), jnp.float32)
-    for array in range(4 * freq_count):
+    for array in range(4 * freqs):
         for buffer in (first, second):
             buffer[array, 0:PAD, :] = zeros
             buffer[array, PAD + grid_rows : 2 * PAD + grid_rows, :] = zeros
@@ -56,11 +60,12 @@
         for own, source in ((0, surf_own), (1, surf_other)):
             line = line_index ^ (2 * reversed_bits(slot, near_count) + own)
             start = pl.multiple_of(PAD + line * row_count, SUB)
-            for array in range(4 * freq_count):
-                block = source[slot, array]
-                if array >= 3 * freq_count:
-                    block = -block
-                first[array, pl.ds(start, row_count), :] = block
+            for kind in range(4):
+                for freq in range(freqs):
+                    block = source[slot, kind, parity * freqs + freq]
+                    if kind == 3:
+                        block = -block
+                    first[kind * freqs + freq, pl.ds(start, row_count), :] = block
 
     lane = lax.broadcasted_iota(jnp.int32, (SUB, width), 1)
     inside = {
@@ -77,13 +82,13 @@
                 own = bins_own[slot, slab_slot, level_index, pl.ds(inner, SUB), :]
                 other = bins_other[slot, slab_slot, level_index, pl.ds(inner, SUB), :]
                 bins = jnp.where((line & 1) == 0, own, other)
-                for freq in range(freq_count):
+                for freq in range(freqs):
                     sums = [None] * 4
                     centre = None
                     for tap in range(taps):
                         coefs = [
                             jnp.take_along_axis(
-                                wide[(tap * 2 + part) * freq_count + freq],
+                                wide[(tap * 2 + part) * freqs + freq],
                                 bins,
                                 axis=1,
                                 mode="promise_in_bounds",
@@ -93,12 +98,8 @@
                         step = TAP_COLS[tap]
                         if step == 0:
                             fields = [
-                                source[
-                                    array * freq_count + freq,
-                                    pl.ds(PAD + row + TAP_ROWS[tap], SUB),
-                                    :,
-                                ]
-                                for array in range(4)
+                                source[kind * freqs + freq, pl.ds(PAD + row + TAP_ROWS[tap], SUB), :]
+                                for kind in range(4)
                             ]
                             if tap == 0:
                                 centre = fields
@@ -116,8 +117,8 @@
                             for part, term in ((0, term_real), (1, term_imag)):
                                 place = 2 * field + part
                                 sums[place] = term if sums[place] is None else sums[place] + term
-                    for array in range(4):
-                        target[array * freq_count + freq, pl.ds(PAD + row, SUB), :] = sums[array]
+                    for kind in range(4):
+                        target[kind * freqs + freq, pl.ds(PAD + row, SUB), :] = sums[kind]
             return carry
 
         lax.fori_loop(0, grid_rows // row_chunk, chunk_step, 0)
@@ -133,21 +134,36 @@
 
     lax.fori_loop(0, depth_index + 1, slab_step, 0)
 
-    base = pl.multiple_of(PAD + line_index * row_count, SUB)
+    tall = row_count + 2 * OFF_Y
+    for out, line in ((mine, line_index), (theirs, line_index ^ 1)):
+        base = pl.multiple_of(PAD + line * row_count, SUB)
+        for array in range(2 * freqs):
+            out[array * row_count : (array + 1) * row_count, :] = first[
+                array, pl.ds(base, row_count), :
+            ]
+            start = 2 * freqs * row_count + array * tall
+            above = pl.multiple_of(base - OFF_Y, SUB)
+            out[start : start + tall, :] = first[2 * freqs + array, pl.ds(above, tall), :]
+
+
+def image_kernel(freqs, offsets, mine, other, image):
+    row_count, width = image.shape[2:]
+    tall = row_count + 2 * OFF_Y
     lanes = lax.broadcasted_iota(jnp.int32, (row_count, width), 1)
-    sources = [first[array, pl.ds(base, row_count), :] for array in range(2 * freq_count)]
-
     for h in range(image.shape[1]):
-        dy = offsets[h, 0]
-        dx = offsets[h, 1]
+        dy = offsets[0, h]
+        dx = offsets[1, h]
         valid = (lanes + dx >= 0) & (lanes + dx < width)
         total = None
-        for array in range(2 * freq_count):
-            value = first[2 * freq_count + array, pl.ds(base + dy, row_count), :]
-            term = sources[array] * pltpu.roll(value, lax.rem(width - dx, width), 1)
-            if array >= freq_count:
-                term = -term
-            total = term if total is None else total + term
+        for pack in (mine, other):
+            for array in range(2 * freqs):
+                source = pack[array * row_count : (array + 1) * row_count, :]
+                start = 2 * freqs * row_count + array * tall + OFF_Y
+                value = pack[pl.ds(start + dy, row_count), :]
+                term = source * pltpu.roll(value, lax.rem(width - dx, width), 1)
+                if array >= freqs:
+                    term = -term
+                total = term if total is None else total + term
         image[0, h] = jnp.where(valid, total, 0.0)
 
 
@@ -156,12 +172,12 @@
     line_count = lax.axis_size("xline")
     row_count = surface_fields.shape[3]
     width = surface_fields.shape[4]
-    freq_count = surface_fields.shape[2]
+    freqs = surface_fields.shape[2] // 2
     levels = velocity_bins.shape[1]
     grid_rows = row_count * line_count
     row_chunk = next(rows for rows in (64, 32, 16, 8) if grid_rows % rows == 0)
 
-    surf = surface_fields.reshape(1, 4 * freq_count, row_count, width)
+    surf = surface_fields.reshape(1, 4, 2 * freqs, row_count, width)
     bins = velocity_bins
     line_bits = bits_of(line_count)[:-1]
     for bit in line_bits:
@@ -174,22 +190,34 @@
     surf_other = swap(surf, "xline", 1)
     bins_other = swap(bins, "xline", 1)
 
-    table = stencil_table.reshape(-1, stencil_table.shape[3])
-    sizes = (depth_count, line_count, levels, row_count, freq_count, row_chunk)
-    field_shape = (4 * freq_count, grid_rows + 2 * PAD, width)
+    sizes = (depth_count, line_count, levels, row_count, freqs, row_chunk)
+    field_shape = (4 * freqs, grid_rows + 2 * PAD, width)
+    pack_rows = 2 * freqs * (2 * row_count + 2 * OFF_Y)
+    pack = jax.ShapeDtypeStruct((pack_rows, width), jnp.float32)
     whole = pl.BlockSpec(memory_space=pltpu.VMEM)
-    return pl.pallas_call(
-        functools.partial(image_kernel, sizes),
-        out_shape=jax.ShapeDtypeStruct((1, offset_list.shape[0], row_count, width), jnp.float32),
-        in_specs=[pl.BlockSpec(memory_space=pltpu.SMEM)] + [whole] * 5,
-        out_specs=whole,
+    cells = 2 * (surf.size + bins.size) + 2 * 4 * freqs * field_shape[1] * width
+    mine, theirs = pl.pallas_call(
+        functools.partial(continuation_kernel, sizes),
+        out_shape=[pack, pack],
+        in_specs=[whole] * 5,
+        out_specs=[whole] * 2,
         scratch_shapes=[
-            pltpu.VMEM((table.shape[0], SUB, width), jnp.float32),
+            pltpu.VMEM((len(TAP_ROWS) * 2 * freqs, SUB, width), jnp.float32),
             pltpu.VMEM(field_shape, jnp.float32),
             pltpu.VMEM(field_shape, jnp.float32),
         ],
+        compiler_params=pltpu.CompilerParams(vmem_limit_bytes=4 * cells + (2 << 20)),
         name="continuation",
-    )(offset_list, table, surf, surf_other, bins, bins_other)
+    )(stencil_table, surf, surf_other, bins, bins_other)
+    other = swap(theirs, "xline", 1)
+    return pl.pallas_call(
+        functools.partial(image_kernel, freqs),
+        out_shape=jax.ShapeDtypeStruct((1, offset_list.shape[0], row_count, width), jnp.float32),
+        in_specs=[pl.BlockSpec(memory_space=pltpu.SMEM), whole, whole],
+        out_specs=whole,
+        compiler_params=pltpu.CompilerParams(vmem_limit_bytes=4 << 20),
+        name="imaging",
+    )(offset_list.T, mine, other)
 
 
 def solution(mesh):

time: 38.9 us -> 32.1 us (0.83)
  Pallas kernels: 15.5 us -> 8.37 us
  local copies, waits for them, and re-layouts: 2.66 us -> 0.69 us
  waiting for transfers between devices: 11.6 us -> 13.5 us
  starting transfers between devices: 8.07 us -> 8.51 us
    pallas_call x1 -> x2, Pallas kernels: 15.5 us -> 8.37 us  [the longest x1 6.95 us: shards(): pl.pallas_call(functools.partial(continuation_kernel, sizes), out_shape=[...]
    ppermute x7 -> x8, waiting for transfers between devices: 11.6 us -> 13.5 us  [swap(): return lax.ppermute(block, axis, [(i, i ^ bit) for i in range(count)])]
    unnamed x17 -> x8, local copies, waits for them, and re-layouts: 2.04 us -> 0.69 us
    reshape x1 -> x0, local copies, waits for them, and re-layouts: 0.62 us -> none  [shards(): table = stencil_table.reshape(-1, stencil_table.shape[3])]
    ppermute x7 -> x8, starting transfers between devices: 8.07 us -> 8.51 us  [swap(): return lax.ppermute(block, axis, [(i, i ^ bit) for i in range(count)])]
  transfers between devices with their start and end apart: 7 -> 8, of which waited for: 4 -> 6; matrix products, arithmetic and copies ran while one was open for 3% -> 0% of each run, Pallas kernels for 0% -> 0%
where the time goes in v2:
time: 32.1 us; the launch traced here: 31.9 us
  waiting for transfers between devices  13.5 us (42%)
  starting transfers between devices  8.51 us (27%)
  Pallas kernels  8.37 us (26%)
  other arithmetic  0.76 us (2%)
  local copies, waits for them, and re-layouts  0.69 us (2%)
    ppermute x8, waiting for transfers between devices, swap(): return lax.ppermute(block, axis, [(i, i ^ bit) for i in range(count)])  13.5 us
    ppermute x8, starting transfers between devices, swap(): return lax.ppermute(block, axis, [(i, i ^ bit) for i in range(count)])  8.51 us
    pallas_call x1, Pallas kernels, shards(): pl.pallas_call(functools.partial(continuation_kernel, sizes), out_shape=[...  6.95 us
    pallas_call x1, Pallas kernels, shards(): pl.pallas_call(functools.partial(image_kernel, freqs), out_shape=jax.Shap...  1.41 us
    concatenate x2, other arithmetic, shards(): bins = jnp.concatenate([bins, swap(bins, 'depth', bit)], axis=0)  0.73 us
    unnamed x8, local copies, waits for them, and re-layouts  0.69 us
  transfers between devices with their start and end apart: 8, of which 6 were waited for; matrix products, arithmetic and copies ran while one was open for 0% of the time, Pallas kernels for 0%

profile of v2, /device:TPU:29, one launch (start us, length us, event | category | flops | bytes accessed | tf_op | source)
XLA Modules:
  0.0 31.9 jit_solution(3569529572234530206)
XLA Ops:
  0.0 0.0 copy-start.2
  0.0 0.1 collective-permute-start.2
  0.1 3.7 %collective-permute-done.2 = s32[1,2,16,128]{3,2,1,0:T(8,128)S(1)} collective-permute-done((s32[1,2,16,128]{3,2,1,0:T(8,128)}, s32[1,2,16,128]{3,2,1,0:T(8,128)S(1)}, u32[]{:S(2)}, u32[]{:S(2)}) %collective-permute-start.2) | collective-permute-done | bytes 16416 | tf_op jit(solution)/shard_map/ppermute | solution.py:20
  3.8 0.7 %pad_add_fusion.2 = s32[2,2,16,128]{3,2,1,0:T(8,128)S(1)} fusion(s32[1,2,16,128]{3,2,1,0:T(8,128)S(1)} %collective-permute-done.2, s32[1,2,16,128]{3,2,1,0:T(8,128)} %param.6), kind=kLoop, calls=%fused_computation.4 | loop fusion | flops 8192 | bytes 65536 | tf_op jit(solution)/shard_map/concatenate | solution.py:186
  4.5 0.1 collective-permute-start.3
  4.6 2.7 %collective-permute-done.3 = s32[2,2,16,128]{3,2,1,0:T(8,128)S(1)} collective-permute-done((s32[2,2,16,128]{3,2,1,0:T(8,128)S(1)}, s32[2,2,16,128]{3,2,1,0:T(8,128)S(1)}, u32[]{:S(2)}, u32[]{:S(2)}) %collective-permute-start.3) | collective-permute-done | bytes 32800 | tf_op jit(solution)/shard_map/ppermute | solution.py:20
  7.3 0.0 copy-done.2
  7.3 0.0 copy-start.3
  7.3 0.3 collective-permute-start.4
  7.6 2.9 %collective-permute-done.4 = s32[4,2,16,128]{3,2,1,0:T(8,128)S(1)} collective-permute-done((s32[4,2,16,128]{3,2,1,0:T(8,128)S(1)}, s32[4,2,16,128]{3,2,1,0:T(8,128)S(1)}, u32[]{:S(2)}, u32[]{:S(2)}) %collective-permute-start.4) | collective-permute-done | bytes 65568 | tf_op jit(solution)/shard_map/ppermute | solution.py:20
  10.5 1.3 %collective-permute-start.5 = (s32[1,8,2,16,128]{4,3,2,1,0:T(8,128)S(1)}, s32[1,8,2,16,128]{4,3,2,1,0:T(8,128)S(1)}, u32[]{:S(2)}, u32[]{:S(2)}) collective-permute-start(s32[1,8,2,16,128]{4,3,2,1,0:T(8,128)S(1)} %add_bitcast_fusion), channel_id=1, source_target_pairs={{0,2},{1,3},{2,0},{3,1},{4,6},{5,7},{6,4},{7,5},{8,10},{9,11},{10,... | collective-permute-start | bytes 393224 | tf_op jit(solution)/shard_map/ppermute | solution.py:20
  11.7 0.0 copy-done.3
  11.7 0.3 collective-permute-start
  12.0 2.3 %collective-permute-done.5 = s32[1,8,2,16,128]{4,3,2,1,0:T(8,128)S(1)} collective-permute-done((s32[1,8,2,16,128]{4,3,2,1,0:T(8,128)S(1)}, s32[1,8,2,16,128]{4,3,2,1,0:T(8,128)S(1)}, u32[]{:S(2)}, u32[]{:S(2)}) %collective-permute-start.5) | collective-permute-done | bytes 131104 | tf_op jit(solution)/shard_map/ppermute | solution.py:20
  14.4 0.0 copy-start
  14.4 5.3 %collective-permute-start.6 = (s32[2,8,2,16,128]{4,3,2,1,0:T(8,128)S(1)}, s32[2,8,2,16,128]{4,3,2,1,0:T(8,128)S(1)}, u32[]{:S(2)}, u32[]{:S(2)}) collective-permute-start(s32[2,8,2,16,128]{4,3,2,1,0:T(8,128)S(1)} %pad_add_fusion.bins_own), channel_id=1, source_target_pairs={{0,1},{1,0},{2,3},{3,2},{4,5},{5,4},{6,7},{7,6},{8,9},{9,8},{10,11... | collective-permute-start | bytes 786440 | tf_op jit(solution)/shard_map/ppermute | solution.py:20
  19.7 0.0 collective-permute-done
  19.7 0.8 %collective-permute-start.1 = (f32[2,4,2,16,128]{4,3,2,1,0:T(8,128)S(1)}, f32[2,4,2,16,128]{4,3,2,1,0:T(8,128)S(1)}, u32[]{:S(2)}, u32[]{:S(2)}) collective-permute-start(f32[2,4,2,16,128]{4,3,2,1,0:T(8,128)S(1)} %pad_maximum_fusion.surf_own), channel_id=1, source_target_pairs={{0,1},{1,0},{2,3},{3,2},{4,5},{5,4},{6,7},{7,6},{8,9},{9,8},{10,11... | collective-permute-start | bytes 393224 | tf_op jit(solution)/shard_map/ppermute | solution.py:20
  20.5 1.0 %collective-permute-done.1.surf_other = f32[2,4,2,16,128]{4,3,2,1,0:T(8,128)S(1)} collective-permute-done((f32[2,4,2,16,128]{4,3,2,1,0:T(8,128)S(1)}, f32[2,4,2,16,128]{4,3,2,1,0:T(8,128)S(1)}, u32[]{:S(2)}, u32[]{:S(2)}) %collective-permute-start.1) | collective-permute-done | bytes 131104 | tf_op jit(solution)/shard_map/ppermute | solution.py:20
  21.5 0.0 collective-permute-done.6.bins_other
  21.5 0.0 copy-done
  21.5 7.0 %continuation.1 = (f32[96,128]{1,0:T(8,128)S(1)}, f32[96,128]{1,0:T(8,128)S(1)}) custom-call(f32[13,2,2,128]{3,2,1,0:T(2,128)S(1)} %copy-done, f32[2,4,2,16,128]{4,3,2,1,0:T(8,128)S(1)} %pad_maximum_fusion.surf_own, f32[2,4,2,16,128]{4,3,2,1,0:T(8,128)S(1)} %collective-permute-done.1.surf_other, s32[2,8,2,16,128]{4,3,2,1,0:T(8,128)S(1)} %pad_add_fusion.bins_own, ...), custom_call_target="tpu_custom_call" | custom-call | tf_op jit(solution)/shard_map/continuation/pallas_call | solution.py:199
  28.4 0.4 %collective-permute-start.7 = (f32[96,128]{1,0:T(8,128)S(1)}, f32[96,128]{1,0:T(8,128)S(1)}, u32[]{:S(2)}, u32[]{:S(2)}) collective-permute-start(f32[96,128]{1,0:T(8,128)S(1)} %get-tuple-element.8), channel_id=1, source_target_pairs={{0,1},{1,0},{2,3},{3,2},{4,5},{5,4},{6,7},{7,6},{8,9},{9,8},{10,11... | collective-permute-start | bytes 147464 | tf_op jit(solution)/shard_map/ppermute | solution.py:20
  28.9 0.9 %collective-permute-done.7.other = f32[96,128]{1,0:T(8,128)S(1)} collective-permute-done((f32[96,128]{1,0:T(8,128)S(1)}, f32[96,128]{1,0:T(8,128)S(1)}, u32[]{:S(2)}, u32[]{:S(2)}) %collective-permute-start.7) | collective-permute-done | bytes 49184 | tf_op jit(solution)/shard_map/ppermute | solution.py:20
  29.8 0.0 copy-start.1
  29.8 0.7 %copy-done.1 = s32[16,2]{0,1:T(2,128)S(1)} copy-done((s32[16,2]{0,1:T(2,128)S(1)}, s32[16,2]{0,1:T(2,128)}, u32[]{:S(2)}) %copy-start.1) | copy-done | bytes 152
  30.4 1.4 %imaging.1 = f32[1,16,16,128]{3,2,1,0:T(8,128)} custom-call(s32[2,16]{1,0:T(2,128)S(1)} %bitcast.4, f32[96,128]{1,0:T(8,128)S(1)} %get-tuple-element.7.mine, f32[96,128]{1,0:T(8,128)S(1)} %collective-permute-done.7.other), custom_call_target="tpu_custom_call" | custom-call | tf_op jit(solution)/shard_map/imaging/pallas_call | solution.py:213
  (4 shorter events, 0.0 us)
Async XLA Ops:
  0.0 7.3 %copy-start.2 = (s32[1,2,16,128]{3,2,1,0:T(8,128)S(1)}, s32[1,2,16,128]{3,2,1,0:T(8,128)}, u32[]{:S(2)}) copy-start(s32[1,2,16,128]{3,2,1,0:T(8,128)} %param.6) | copy-start | bytes 49156
  0.0 3.8 %collective-permute-start.2 = (s32[1,2,16,128]{3,2,1,0:T(8,128)}, s32[1,2,16,128]{3,2,1,0:T(8,128)S(1)}, u32[]{:S(2)}, u32[]{:S(2)}) collective-permute-start(s32[1,2,16,128]{3,2,1,0:T(8,128)} %param.6), channel_id=1, source_target_pairs={{0,16},{4,20},{8,24},{12,28},{16,0},{20,4},{24,8},{28,12},{1,17},{... | collective-permute-start | bytes 49160 | tf_op jit(solution)/shard_map/ppermute | solution.py:20
  4.5 2.8 %collective-permute-start.3 = (s32[2,2,16,128]{3,2,1,0:T(8,128)S(1)}, s32[2,2,16,128]{3,2,1,0:T(8,128)S(1)}, u32[]{:S(2)}, u32[]{:S(2)}) collective-permute-start(s32[2,2,16,128]{3,2,1,0:T(8,128)S(1)} %pad_add_fusion.2), channel_id=1, source_target_pairs={{0,8},{4,12},{8,0},{12,4},{16,24},{20,28},{24,16},{28,20},{1,9},{5... | collective-permute-start | bytes 98312 | tf_op jit(solution)/shard_map/ppermute | solution.py:20
  7.3 4.5 %copy-start.3 = (f32[2,2,2,16,128]{4,3,2,1,0:T(8,128)S(1)}, f32[2,2,2,16,128]{4,3,2,1,0:T(8,128)}, u32[]{:S(2)}) copy-start(f32[2,2,2,16,128]{4,3,2,1,0:T(8,128)} %param.4) | copy-start | bytes 196612
  7.3 3.2 %collective-permute-start.4 = (s32[4,2,16,128]{3,2,1,0:T(8,128)S(1)}, s32[4,2,16,128]{3,2,1,0:T(8,128)S(1)}, u32[]{:S(2)}, u32[]{:S(2)}) collective-permute-start(s32[4,2,16,128]{3,2,1,0:T(8,128)S(1)} %pad_add_fusion.1), channel_id=1, source_target_pairs={{0,4},{4,0},{8,12},{12,8},{16,20},{20,16},{24,28},{28,24},{1,5},{5... | collective-permute-start | bytes 196616 | tf_op jit(solution)/shard_map/ppermute | solution.py:20
  10.5 3.9 %collective-permute-start.5 = (s32[1,8,2,16,128]{4,3,2,1,0:T(8,128)S(1)}, s32[1,8,2,16,128]{4,3,2,1,0:T(8,128)S(1)}, u32[]{:S(2)}, u32[]{:S(2)}) collective-permute-start(s32[1,8,2,16,128]{4,3,2,1,0:T(8,128)S(1)} %add_bitcast_fusion), channel_id=1, source_target_pairs={{0,2},{1,3},{2,0},{3,1},{4,6},{5,7},{6,4},{7,5},{8,10},{9,11},{10,... | collective-permute-start | bytes 393224 | tf_op jit(solution)/shard_map/ppermute | solution.py:20
  11.7 8.0 %collective-permute-start = (f32[1,4,2,16,128]{4,3,2,1,0:T(8,128)S(1)}, f32[1,4,2,16,128]{4,3,2,1,0:T(8,128)S(1)}, u32[]{:S(2)}, u32[]{:S(2)}) collective-permute-start(f32[1,4,2,16,128]{4,3,2,1,0:T(8,128)S(1)} %bitcast.5), channel_id=1, source_target_pairs={{0,2},{1,3},{2,0},{3,1},{4,6},{5,7},{6,4},{7,5},{8,10},{9,11},{10,... | collective-permute-start | bytes 196616 | tf_op jit(solution)/shard_map/ppermute | solution.py:20
  14.4 7.1 %copy-start = (f32[13,2,2,128]{3,2,1,0:T(2,128)S(1)}, f32[13,2,2,128]{3,2,1,0:T(2,128)}, u32[]{:S(2)}) copy-start(f32[13,2,2,128]{3,2,1,0:T(2,128)} %table.1) | copy-start | bytes 79876
  14.4 7.1 %collective-permute-start.6 = (s32[2,8,2,16,128]{4,3,2,1,0:T(8,128)S(1)}, s32[2,8,2,16,128]{4,3,2,1,0:T(8,128)S(1)}, u32[]{:S(2)}, u32[]{:S(2)}) collective-permute-start(s32[2,8,2,16,128]{4,3,2,1,0:T(8,128)S(1)} %pad_add_fusion.bins_own), channel_id=1, source_target_pairs={{0,1},{1,0},{2,3},{3,2},{4,5},{5,4},{6,7},{7,6},{8,9},{9,8},{10,11... | collective-permute-start | bytes 786440 | tf_op jit(solution)/shard_map/ppermute | solution.py:20
  19.7 1.7 %collective-permute-start.1 = (f32[2,4,2,16,128]{4,3,2,1,0:T(8,128)S(1)}, f32[2,4,2,16,128]{4,3,2,1,0:T(8,128)S(1)}, u32[]{:S(2)}, u32[]{:S(2)}) collective-permute-start(f32[2,4,2,16,128]{4,3,2,1,0:T(8,128)S(1)} %pad_maximum_fusion.surf_own), channel_id=1, source_target_pairs={{0,1},{1,0},{2,3},{3,2},{4,5},{5,4},{6,7},{7,6},{8,9},{9,8},{10,11... | collective-permute-start | bytes 393224 | tf_op jit(solution)/shard_map/ppermute | solution.py:20
  28.4 1.3 %collective-permute-start.7 = (f32[96,128]{1,0:T(8,128)S(1)}, f32[96,128]{1,0:T(8,128)S(1)}, u32[]{:S(2)}, u32[]{:S(2)}) collective-permute-start(f32[96,128]{1,0:T(8,128)S(1)} %get-tuple-element.8), channel_id=1, source_target_pairs={{0,1},{1,0},{2,3},{3,2},{4,5},{5,4},{6,7},{7,6},{8,9},{9,8},{10,11... | collective-permute-start | bytes 147464 | tf_op jit(solution)/shard_map/ppermute | solution.py:20
  29.8 0.7 %copy-start.1 = (s32[16,2]{0,1:T(2,128)S(1)}, s32[16,2]{0,1:T(2,128)}, u32[]{:S(2)}) copy-start(s32[16,2]{0,1:T(2,128)} %param.7) | copy-start | bytes 388

commit v3 on v2

v3 whole, which is shorter than its diff:
```python
import functools

import jax
import jax.numpy as jnp
from jax import lax
from jax.experimental import pallas as pl
from jax.experimental.pallas import tpu as pltpu
from jax.sharding import PartitionSpec as P

OFF_Y = 8
TAP_ROWS = (0, -4, -3, -2, -1, 1, 2, 3, 4, 0, 0, 0, 0)
TAP_COLS = (0, 0, 0, 0, 0, 0, 0, 0, 0, -2, -1, 1, 2)
PAD = 8
SUB = 8
VMEM = pl.BlockSpec(memory_space=pltpu.VMEM)


def bits_of(count):
    return [1 << k for k in reversed(range(count.bit_length() - 1))]


def reversed_bits(value, count):
    width = count.bit_length() - 1
    total = 0
    for k in range(width):
        total = total + (((value >> k) & 1) << (width - 1 - k))
    return total


def odd_bits(value, count):
    width = count.bit_length() - 1
    total = 0
    for k in range(width):
        total = total ^ ((value >> k) & 1)
    return total


def hop(block, depth_bit, line_bit):
    depths, lines = lax.axis_size("depth"), lax.axis_size("xline")
    route = [
        (d * lines + x, (d ^ depth_bit) * lines + (x ^ line_bit))
        for d in range(depths)
        for x in range(lines)
    ]
    return lax.ppermute(block, ("depth", "xline"), route)


def stage_kernel(freqs, table, bins, surf, offsets, wide, bins_out, surf_out, offsets_out):
    parity = lax.axis_index("xline") & 1
    width = surf.shape[-1]
    bins_out[...] = bins[...]
    offsets_out[...] = offsets[...]
    for kind in range(4):
        block = surf[0, kind]
        surf_out[0, kind] = -block if kind == 3 else block
    for tap in range(len(TAP_ROWS)):
        for part in range(2):
            for freq in range(freqs):
                row = table[tap, part, pl.ds(parity * freqs + freq, 1), :]
                wide[(tap * 2 + part) * freqs + freq] = jnp.broadcast_to(row, (SUB, width))


def clear_edges(buffer):
    count, rows, width = buffer.shape
    zeros = jnp.zeros((PAD, width), jnp.float32)
    for array in range(count):
        buffer[array, 0:PAD, :] = zeros
        buffer[array, rows - PAD : rows, :] = zeros


def run_slabs(sizes, start, stop, wide, bins_own, bins_other, first, second):
    depth_count, line_count, levels, row_count, freqs, row_chunk = sizes
    depth_index = lax.axis_index("depth")
    line_index = lax.axis_index("xline")
    width = wide.shape[2]
    grid_rows = row_count * line_count
    near_count = line_count // 2
    lane = lax.broadcasted_iota(jnp.int32, (SUB, width), 1)
    inside = {
        step: (lane + step >= 0) & (lane + step < width) for step in sorted(set(TAP_COLS) - {0})
    }

    def level(slot, odd, level_index, source, target):
        def chunk_step(chunk, carry):
            for block in range(row_chunk // SUB):
                row = pl.multiple_of(chunk * row_chunk + block * SUB, SUB)
                line = (row // row_count) ^ line_index
                near = reversed_bits(line >> 1, near_count)
                inner = pl.multiple_of(row % row_count, SUB)
                own = bins_own[near, slot, level_index, pl.ds(inner, SUB), :]
                other = bins_other[near, slot, level_index, pl.ds(inner, SUB), :]
                crossed = odd ^ odd_bits(line >> 1, near_count)
                bins = jnp.where((line & 1) == crossed, own, other)
                for freq in range(freqs):
                    sums = [None] * 4
                    centre = None
                    for tap in range(len(TAP_ROWS)):
                        coefs = [
                            jnp.take_along_axis(
                                wide[(tap * 2 + part) * freqs + freq],
                                bins,
                                axis=1,
                                mode="promise_in_bounds",
                            )
                            for part in range(2)
                        ]
                        step = TAP_COLS[tap]
                        if step == 0:
                            fields = [
                                source[kind * freqs + freq, pl.ds(PAD + row + TAP_ROWS[tap], SUB), :]
                                for kind in range(4)
                            ]
                            if tap == 0:
                                centre = fields
                        else:
                            fields = [
                                jnp.where(
                                    inside[step], pltpu.roll(value, (-step) % width, 1), 0.0
                                )
                                for value in centre
                            ]
                        for field in range(2):
                            real, imag = fields[2 * field], fields[2 * field + 1]
                            term_real = coefs[0] * real - coefs[1] * imag
                            term_imag = coefs[0] * imag + coefs[1] * real
                            for part, term in ((0, term_real), (1, term_imag)):
                                place = 2 * field + part
                                sums[place] = term if sums[place] is None else sums[place] + term
                    for kind in range(4):
                        target[kind * freqs + freq, pl.ds(PAD + row, SUB), :] = sums[kind]
            return carry

        lax.fori_loop(0, grid_rows // row_chunk, chunk_step, 0)

    def slab_step(slab, carry):
        apart = slab ^ depth_index
        slot = reversed_bits(apart & (depth_count // 2 - 1), depth_count // 2)
        odd = odd_bits(apart, depth_count)
        buffers = (first, second)
        for level_index in range(levels):
            level(slot, odd, level_index, buffers[level_index % 2], buffers[1 - level_index % 2])
        if levels % 2:
            first[...] = second[...]
        return carry

    lax.fori_loop(start, stop, slab_step, 0)


def upper_kernel(sizes, wide, surf_own, surf_other, bins_own, bins_other, state, second):
    depth_count, line_count, _, row_count, freqs, _ = sizes
    depth_index = lax.axis_index("depth")
    line_index = lax.axis_index("xline")
    near_count = line_count // 2
    clear_edges(state)
    clear_edges(second)
    for near in range(near_count):
        odd = near.bit_count() & 1
        for own, source in ((odd, surf_own), (1 - odd, surf_other)):
            line = line_index ^ (2 * reversed_bits(near, near_count) + own)
            start = pl.multiple_of(PAD + line * row_count, SUB)
            for kind in range(4):
                for freq in range(freqs):
                    block = source[near, kind, (line_index & 1) * freqs + freq]
                    state[kind * freqs + freq, pl.ds(start, row_count), :] = block
    half = depth_count // 2
    stop = jnp.where(depth_index >= half, half, 0)
    run_slabs(sizes, 0, stop, wide, bins_own, bins_other, state, second)


def lower_kernel(sizes, wide, bins_own, bins_other, state, mine, theirs, first, second):
    depth_count, _, _, row_count, freqs, _ = sizes
    depth_index = lax.axis_index("depth")
    line_index = lax.axis_index("xline")
    first[...] = state[...]
    clear_edges(second)
    half = depth_count // 2
    start = jnp.where(depth_index >= half, half, 0)
    run_slabs(sizes, start, depth_index + 1, wide, bins_own, bins_other, first, second)
    tall = row_count + 2 * OFF_Y
    for out, line in ((mine, line_index), (theirs, line_index ^ 1)):
        base = pl.multiple_of(PAD + line * row_count, SUB)
        for array in range(2 * freqs):
            out[array * row_count : (array + 1) * row_count, :] = first[
                array, pl.ds(base, row_count), :
            ]
            below = 2 * freqs * row_count + array * tall
            above = pl.multiple_of(base - OFF_Y, SUB)
            out[below : below + tall, :] = first[2 * freqs + array, pl.ds(above, tall), :]


def image_kernel(freqs, offsets, mine, other, image):
    row_count, width = image.shape[2:]
    tall = row_count + 2 * OFF_Y
    lanes = lax.broadcasted_iota(jnp.int32, (row_count, width), 1)
    for h in range(image.shape[1]):
        dy = offsets[0, h]
        dx = offsets[1, h]
        valid = (lanes + dx >= 0) & (lanes + dx < width)
        total = None
        for pack in (mine, other):
            for array in range(2 * freqs):
                source = pack[array * row_count : (array + 1) * row_count, :]
                start = 2 * freqs * row_count + array * tall + OFF_Y
                value = pack[pl.ds(start + dy, row_count), :]
                term = source * pltpu.roll(value, lax.rem(width - dx, width), 1)
                if array >= freqs:
                    term = -term
                total = term if total is None else total + term
        image[0, h] = jnp.where(valid, total, 0.0)


def shards(surface_fields, stencil_table, velocity_bins, offset_list):
    depth_count = lax.axis_size("depth")
    line_count = lax.axis_size("xline")
    row_count = surface_fields.shape[3]
    width = surface_fields.shape[4]
    freqs = surface_fields.shape[2] // 2
    levels = velocity_bins.shape[1]
    grid_rows = row_count * line_count
    row_chunk = next(rows for rows in (64, 32, 16, 8) if grid_rows % rows == 0)
    sizes = (depth_count, line_count, levels, row_count, freqs, row_chunk)
    depth_bits = bits_of(depth_count)
    line_bits = bits_of(line_count)[:-1]
    f32 = jnp.float32

    def call(kernel, outs, scratch, flops, *args):
        size = sum(array.size for array in (*args, *outs)) + sum(ref.shape[0] * ref.shape[1] * ref.shape[2] for ref in scratch)
        return pl.pallas_call(
            kernel,
            out_shape=outs,
            in_specs=[VMEM] * len(args),
            out_specs=[VMEM] * len(outs),
            scratch_shapes=scratch,
            compiler_params=pltpu.CompilerParams(vmem_limit_bytes=4 * size + (2 << 20)),
            cost_estimate=pl.CostEstimate(flops=flops, bytes_accessed=4 * size, transcendentals=0),
        )(*args)

    surf = surface_fields.reshape(1, 4, 2 * freqs, row_count, width)
    offsets = offset_list.T
    like = jax.ShapeDtypeStruct
    wide, bins, surf, offsets = call(
        functools.partial(stage_kernel, freqs),
        [
            like((len(TAP_ROWS) * 2 * freqs, SUB, width), f32),
            like(velocity_bins.shape, velocity_bins.dtype),
            like(surf.shape, f32),
            like(offsets.shape, offsets.dtype),
        ],
        [],
        1000,
        stencil_table,
        velocity_bins,
        surf,
        offsets,
    )

    far = hop(velocity_bins, depth_bits[0], 1)
    near = bins
    for bit in line_bits:
        surf = jnp.concatenate([surf, hop(surf, 0, bit | 1)], axis=0)
    for bit in depth_bits[1:-1]:
        both = hop(jnp.concatenate([far, near], axis=0), bit, 1)
        count = far.shape[0]
        far = jnp.concatenate([far, both[:count]], axis=0)
        near = jnp.concatenate([near, both[count:]], axis=0)
    surf_other = hop(surf, 0, 1)
    far = jnp.concatenate([far, hop(far, depth_bits[-1], 1)], axis=0)[None]
    near = jnp.concatenate([near, hop(near, depth_bits[-1], 1)], axis=0)[None]
    for bit in line_bits:
        far = jnp.concatenate([far, hop(far, 0, bit | 1)], axis=0)
        near = jnp.concatenate([near, hop(near, 0, bit | 1)], axis=0)
    far_other = hop(far, 0, 1)
    near_other = hop(near, 0, 1)

    field_shape = (4 * freqs, grid_rows + 2 * PAD, width)
    field = pltpu.VMEM(field_shape, f32)
    work = depth_count * levels * len(TAP_ROWS) * 8 * field_shape[0] * grid_rows * width
    (state,) = call(
        functools.partial(upper_kernel, sizes),
        [like(field_shape, f32)],
        [field],
        work // 2,
        wide,
        surf,
        surf_other,
        far,
        far_other,
    )
    pack = like((2 * freqs * (2 * row_count + 2 * OFF_Y), width), f32)
    mine, theirs = call(
        functools.partial(lower_kernel, sizes),
        [pack, pack],
        [field, field],
        work // 2,
        wide,
        near,
        near_other,
        state,
    )
    other = hop(theirs, 0, 1)
    image = pl.pallas_call(
        functools.partial(image_kernel, freqs),
        out_shape=like((1, offset_list.shape[0], row_count, width), f32),
        in_specs=[pl.BlockSpec(memory_space=pltpu.SMEM), VMEM, VMEM],
        out_specs=VMEM,
        compiler_params=pltpu.CompilerParams(vmem_limit_bytes=4 << 20),
        name="imaging",
    )(offsets, mine, other)
    return image


def solution(mesh):
    return jax.shard_map(
        shards,
        mesh=mesh,
        in_specs=(P(None, None, None, "xline", None), P(), P("depth", None, "xline", None), P()),
        out_specs=P("depth", None, "xline", None),
        check_vma=False,
    )
```

time: 32.1 us -> 28.7 us (0.89)
  waiting for transfers between devices: 13.5 us -> 9.43 us
  local copies, waits for them, and re-layouts: 0.69 us -> 2.99 us
  starting transfers between devices: 8.51 us -> 7.37 us
  other arithmetic: 0.76 us -> 0.04 us
    ppermute x8 -> x11, waiting for transfers between devices: 13.5 us -> 9.43 us  [hop(): return lax.ppermute(block, ('depth', 'xline'), route)]
    unnamed x8 -> x9, local copies, waits for them, and re-layouts: 0.69 us -> 2.98 us
    ppermute x8 -> x11, starting transfers between devices: 8.51 us -> 7.37 us  [hop(): return lax.ppermute(block, ('depth', 'xline'), route)]
    concatenate x4 -> x5, other arithmetic: 0.75 us -> 0.03 us  [the longest x1 0.01 us: shards(): far = jnp.concatenate([far, hop(far, 0, bit | 1)], axis=0)]
    pallas_call x2 -> x4, Pallas kernels: 8.37 us -> 8.54 us  [the longest x3 7.13 us: call(): pl.pallas_call(kernel, out_shape=outs, in_specs=[VMEM] * len(args), out_s...]
  transfers between devices with their start and end apart: 8 -> 11, of which waited for: 6 -> 6; matrix products, arithmetic and copies ran while one was open for 0% -> 0% of each run, Pallas kernels for 0% -> 13%
where the time goes in v3:
time: 28.7 us; the launch traced here: 28.4 us
  waiting for transfers between devices  9.43 us (33%)
  Pallas kernels  8.54 us (30%)
  starting transfers between devices  7.37 us (26%)
  local copies, waits for them, and re-layouts  2.99 us (10%)
    ppermute x11, waiting for transfers between devices, hop(): return lax.ppermute(block, ('depth', 'xline'), route)  9.43 us
    ppermute x11, starting transfers between devices, hop(): return lax.ppermute(block, ('depth', 'xline'), route)  7.37 us
    pallas_call x3, Pallas kernels, call(): pl.pallas_call(kernel, out_shape=outs, in_specs=[VMEM] * len(args), out_s...  7.13 us
    unnamed x9, local copies, waits for them, and re-layouts  2.98 us
    pallas_call x1, Pallas kernels, shards(): pl.pallas_call(functools.partial(image_kernel, freqs), out_shape=like((1,...  1.42 us
  transfers between devices with their start and end apart: 11, of which 6 were waited for; matrix products, arithmetic and copies ran while one was open for 0% of the time, Pallas kernels for 13%

profile of v3, /device:TPU:29, one launch (start us, length us, event | category | flops | bytes accessed | tf_op | source)
XLA Modules:
  0.0 28.4 jit_solution(3720691865892463811)
XLA Ops:
  0.0 0.6 %collective-permute-start = (s32[1,2,16,128]{3,2,1,0:T(8,128)}, s32[1,2,16,128]{3,2,1,0:T(8,128)S(1)}, u32[]{:S(2)}, u32[]{:S(2)}) collective-permute-start(s32[1,2,16,128]{3,2,1,0:T(8,128)} %bins.1), channel_id=1, source_target_pairs={{0,17},{1,16},{2,19},{3,18},{4,21},{5,20},{6,23},{7,22},{8,25},{9,... | collective-permute-start | bytes 49160 | tf_op jit(solution)/shard_map/ppermute | solution.py:45
  0.6 0.0 copy-start.3
  0.6 0.7 %copy-done.3 = s32[16,2]{0,1:T(2,128)S(1)} copy-done((s32[16,2]{0,1:T(2,128)S(1)}, s32[16,2]{0,1:T(2,128)}, u32[]{:S(2)}) %copy-start.3) | copy-done | bytes 152
  1.3 0.0 copy-start
  1.3 0.8 %copy-done = f32[2,2,2,16,128]{4,3,2,1,0:T(8,128)S(1)} copy-done((f32[2,2,2,16,128]{4,3,2,1,0:T(8,128)S(1)}, f32[2,2,2,16,128]{4,3,2,1,0:T(8,128)}, u32[]{:S(2)}) %copy-start) | copy-done | bytes 65560
  2.1 0.0 copy-start.1
  2.1 0.7 %copy-done.1 = f32[13,2,2,128]{3,2,1,0:T(2,128)S(1)} copy-done((f32[13,2,2,128]{3,2,1,0:T(2,128)S(1)}, f32[13,2,2,128]{3,2,1,0:T(2,128)}, u32[]{:S(2)}) %copy-start.1) | copy-done | bytes 26648
  2.9 0.0 copy-start.2
  2.9 0.7 %copy-done.2 = s32[1,2,16,128]{3,2,1,0:T(8,128)S(1)} copy-done((s32[1,2,16,128]{3,2,1,0:T(8,128)S(1)}, s32[1,2,16,128]{3,2,1,0:T(8,128)}, u32[]{:S(2)}) %copy-start.2) | copy-done | bytes 16408
  3.6 1.2 %collective-permute-start.5 = (f32[1,4,2,16,128]{4,3,2,1,0:T(8,128)S(1)}, f32[1,4,2,16,128]{4,3,2,1,0:T(8,128)S(1)}, u32[]{:S(2)}, u32[]{:S(2)}) collective-permute-start(f32[1,4,2,16,128]{4,3,2,1,0:T(8,128)S(1)} %get-tuple-element.14), channel_id=1, source_target_pairs={{0,3},{1,2},{2,1},{3,0},{4,7},{5,6},{6,5},{7,4},{8,11},{9,10},{10,... | collective-permute-start | bytes 196616 | tf_op jit(solution)/shard_map/ppermute | solution.py:45
  4.8 0.1 collective-permute-done
  5.0 0.4 %collective-permute-start.1 = (s32[2,2,16,128]{3,2,1,0:T(8,128)S(1)}, s32[2,2,16,128]{3,2,1,0:T(8,128)S(1)}, u32[]{:S(2)}, u32[]{:S(2)}) collective-permute-start(s32[2,2,16,128]{3,2,1,0:T(8,128)S(1)} %pad_add_fusion.3), channel_id=1, source_target_pairs={{0,9},{1,8},{2,11},{3,10},{4,13},{5,12},{6,15},{7,14},{8,1},{9,0},... | collective-permute-start | bytes 98312 | tf_op jit(solution)/shard_map/ppermute | solution.py:45
  5.4 3.0 %collective-permute-done.1 = s32[2,2,16,128]{3,2,1,0:T(8,128)S(1)} collective-permute-done((s32[2,2,16,128]{3,2,1,0:T(8,128)S(1)}, s32[2,2,16,128]{3,2,1,0:T(8,128)S(1)}, u32[]{:S(2)}, u32[]{:S(2)}) %collective-permute-start.1) | collective-permute-done | bytes 32800 | tf_op jit(solution)/shard_map/ppermute | solution.py:45
  8.4 0.6 %collective-permute-start.7 = (s32[2,2,16,128]{3,2,1,0:T(8,128)S(1)}, s32[2,2,16,128]{3,2,1,0:T(8,128)S(1)}, u32[]{:S(2)}, u32[]{:S(2)}) collective-permute-start(s32[2,2,16,128]{3,2,1,0:T(8,128)S(1)} %pad_add_fusion.2), channel_id=1, source_target_pairs={{0,5},{1,4},{2,7},{3,6},{4,1},{5,0},{6,3},{7,2},{8,13},{9,12},{10,... | collective-permute-start | bytes 98312 | tf_op jit(solution)/shard_map/ppermute | solution.py:45
  9.0 1.2 %collective-permute-start.2 = (s32[2,2,16,128]{3,2,1,0:T(8,128)S(1)}, s32[2,2,16,128]{3,2,1,0:T(8,128)S(1)}, u32[]{:S(2)}, u32[]{:S(2)}) collective-permute-start(s32[2,2,16,128]{3,2,1,0:T(8,128)S(1)} %pad_add_fusion.4), channel_id=1, source_target_pairs={{0,5},{1,4},{2,7},{3,6},{4,1},{5,0},{6,3},{7,2},{8,13},{9,12},{10,... | collective-permute-start | bytes 98312 | tf_op jit(solution)/shard_map/ppermute | solution.py:45
  10.2 0.0 collective-permute-done.5
  10.2 0.5 %collective-permute-start.6 = (f32[2,4,2,16,128]{4,3,2,1,0:T(8,128)S(1)}, f32[2,4,2,16,128]{4,3,2,1,0:T(8,128)S(1)}, u32[]{:S(2)}, u32[]{:S(2)}) collective-permute-start(f32[2,4,2,16,128]{4,3,2,1,0:T(8,128)S(1)} %constant_dynamic-update-slice_fusion.surf_own), channel_id=1, source_target_pairs={{0,1},{1,0},{2,3},{3,2},{4,5},{5,4},{6,7},{7,6},{8,9},{9,8},{10,11... | collective-permute-start | bytes 393224 | tf_op jit(solution)/shard_map/ppermute | solution.py:45
  10.7 1.8 %collective-permute-done.7 = s32[2,2,16,128]{3,2,1,0:T(8,128)S(1)} collective-permute-done((s32[2,2,16,128]{3,2,1,0:T(8,128)S(1)}, s32[2,2,16,128]{3,2,1,0:T(8,128)S(1)}, u32[]{:S(2)}, u32[]{:S(2)}) %collective-permute-start.7) | collective-permute-done | bytes 32800 | tf_op jit(solution)/shard_map/ppermute | solution.py:45
  12.4 0.9 %collective-permute-start.8 = (s32[1,4,2,16,128]{4,3,2,1,0:T(8,128)S(1)}, s32[1,4,2,16,128]{4,3,2,1,0:T(8,128)S(1)}, u32[]{:S(2)}, u32[]{:S(2)}) collective-permute-start(s32[1,4,2,16,128]{4,3,2,1,0:T(8,128)S(1)} %add_bitcast_fusion.1), channel_id=1, source_target_pairs={{0,3},{1,2},{2,1},{3,0},{4,7},{5,6},{6,5},{7,4},{8,11},{9,10},{10,... | collective-permute-start | bytes 196616 | tf_op jit(solution)/shard_map/ppermute | solution.py:45
  13.3 0.0 collective-permute-done.2
  13.3 0.9 %collective-permute-start.3 = (s32[1,4,2,16,128]{4,3,2,1,0:T(8,128)S(1)}, s32[1,4,2,16,128]{4,3,2,1,0:T(8,128)S(1)}, u32[]{:S(2)}, u32[]{:S(2)}) collective-permute-start(s32[1,4,2,16,128]{4,3,2,1,0:T(8,128)S(1)} %add_bitcast_fusion), channel_id=1, source_target_pairs={{0,3},{1,2},{2,1},{3,0},{4,7},{5,6},{6,5},{7,4},{8,11},{9,10},{10,... | collective-permute-start | bytes 196616 | tf_op jit(solution)/shard_map/ppermute | solution.py:45
  14.3 1.9 %collective-permute-done.8 = s32[1,4,2,16,128]{4,3,2,1,0:T(8,128)S(1)} collective-permute-done((s32[1,4,2,16,128]{4,3,2,1,0:T(8,128)S(1)}, s32[1,4,2,16,128]{4,3,2,1,0:T(8,128)S(1)}, u32[]{:S(2)}, u32[]{:S(2)}) %collective-permute-start.8) | collective-permute-done | bytes 65568 | tf_op jit(solution)/shard_map/ppermute | solution.py:45
  16.1 0.4 %collective-permute-start.9 = (s32[2,4,2,16,128]{4,3,2,1,0:T(8,128)S(1)}, s32[2,4,2,16,128]{4,3,2,1,0:T(8,128)S(1)}, u32[]{:S(2)}, u32[]{:S(2)}) collective-permute-start(s32[2,4,2,16,128]{4,3,2,1,0:T(8,128)S(1)} %pad_add_fusion.1.bins_own), channel_id=1, source_target_pairs={{0,1},{1,0},{2,3},{3,2},{4,5},{5,4},{6,7},{7,6},{8,9},{9,8},{10,11... | collective-permute-start | bytes 393224 | tf_op jit(solution)/shard_map/ppermute | solution.py:45
  16.6 1.5 %collective-permute-done.3 = s32[1,4,2,16,128]{4,3,2,1,0:T(8,128)S(1)} collective-permute-done((s32[1,4,2,16,128]{4,3,2,1,0:T(8,128)S(1)}, s32[1,4,2,16,128]{4,3,2,1,0:T(8,128)S(1)}, u32[]{:S(2)}, u32[]{:S(2)}) %collective-permute-start.3) | collective-permute-done | bytes 65568 | tf_op jit(solution)/shard_map/ppermute | solution.py:45
  18.1 0.5 %collective-permute-start.4 = (s32[2,4,2,16,128]{4,3,2,1,0:T(8,128)S(1)}, s32[2,4,2,16,128]{4,3,2,1,0:T(8,128)S(1)}, u32[]{:S(2)}, u32[]{:S(2)}) collective-permute-start(s32[2,4,2,16,128]{4,3,2,1,0:T(8,128)S(1)} %pad_add_fusion.bins_own), channel_id=1, source_target_pairs={{0,1},{1,0},{2,3},{3,2},{4,5},{5,4},{6,7},{7,6},{8,9},{9,8},{10,11... | collective-permute-start | bytes 393224 | tf_op jit(solution)/shard_map/ppermute | solution.py:45
  18.6 0.0 collective-permute-done.6.surf_other
  18.6 0.0 collective-permute-done.9.bins_other
  18.6 3.5 %shard_map.47.state = f32[4,80,128]{2,1,0:T(8,128)S(1)} custom-call(f32[26,8,128]{2,1,0:T(8,128)S(1)} %get-tuple-element.12.wide, f32[2,4,2,16,128]{4,3,2,1,0:T(8,128)S(1)} %constant_dynamic-update-slice_fusion.surf_own, f32[2,4,2,16,128]{4,3,2,1,0:T(8,128)S(1)} %collective-permute-done.6.surf_other, s32[2,4,2,16,128]{4,3,2,1,0:T(8,128)S(1)} %pad_add_fusion.1.bins_own, ...), custom_call_target="tpu_custom_call" | custom-call | flops 27262976 | bytes 958464 | tf_op jit(solution)/shard_map/pallas_call | solution.py:228
  22.1 0.0 collective-permute-done.4.bins_other
  22.1 3.6 %shard_map.48 = (f32[96,128]{1,0:T(8,128)S(1)}, f32[96,128]{1,0:T(8,128)S(1)}) custom-call(f32[26,8,128]{2,1,0:T(8,128)S(1)} %get-tuple-element.12.wide, s32[2,4,2,16,128]{4,3,2,1,0:T(8,128)S(1)} %pad_add_fusion.bins_own, s32[2,4,2,16,128]{4,3,2,1,0:T(8,128)S(1)} %collective-permute-done.4.bins_other, f32[4,80,128]{2,1,0:T(8,128)S(1)} %shard_map.47.state), custom_call_target="tpu_custom_call" | custom-call | flops 27262976 | bytes 958464 | tf_op jit(solution)/shard_map/pallas_call | solution.py:228
  25.7 0.2 collective-permute-start.10
  25.9 1.1 %collective-permute-done.10.other = f32[96,128]{1,0:T(8,128)S(1)} collective-permute-done((f32[96,128]{1,0:T(8,128)S(1)}, f32[96,128]{1,0:T(8,128)S(1)}, u32[]{:S(2)}, u32[]{:S(2)}) %collective-permute-start.10) | collective-permute-done | bytes 49184 | tf_op jit(solution)/shard_map/ppermute | solution.py:45
  27.0 1.4 %imaging.1 = f32[1,16,16,128]{3,2,1,0:T(8,128)} custom-call(s32[2,16]{1,0:T(2,128)S(1)} %get-tuple-element.11.offsets, f32[96,128]{1,0:T(8,128)S(1)} %get-tuple-element.15.mine, f32[96,128]{1,0:T(8,128)S(1)} %collective-permute-done.10.other), custom_call_target="tpu_custom_call" | custom-call | tf_op jit(solution)/shard_map/imaging/pallas_call | solution.py:301
  (11 shorter events, 0.1 us)
Async XLA Ops:
  0.0 5.0 %collective-permute-start = (s32[1,2,16,128]{3,2,1,0:T(8,128)}, s32[1,2,16,128]{3,2,1,0:T(8,128)S(1)}, u32[]{:S(2)}, u32[]{:S(2)}) collective-permute-start(s32[1,2,16,128]{3,2,1,0:T(8,128)} %bins.1), channel_id=1, source_target_pairs={{0,17},{1,16},{2,19},{3,18},{4,21},{5,20},{6,23},{7,22},{8,25},{9,... | collective-permute-start | bytes 49160 | tf_op jit(solution)/shard_map/ppermute | solution.py:45
  0.6 0.7 %copy-start.3 = (s32[16,2]{0,1:T(2,128)S(1)}, s32[16,2]{0,1:T(2,128)}, u32[]{:S(2)}) copy-start(s32[16,2]{0,1:T(2,128)} %param.7) | copy-start | bytes 388
  1.3 0.8 %copy-start = (f32[2,2,2,16,128]{4,3,2,1,0:T(8,128)S(1)}, f32[2,2,2,16,128]{4,3,2,1,0:T(8,128)}, u32[]{:S(2)}) copy-start(f32[2,2,2,16,128]{4,3,2,1,0:T(8,128)} %param.4) | copy-start | bytes 196612
  2.1 0.7 %copy-start.1 = (f32[13,2,2,128]{3,2,1,0:T(2,128)S(1)}, f32[13,2,2,128]{3,2,1,0:T(2,128)}, u32[]{:S(2)}) copy-start(f32[13,2,2,128]{3,2,1,0:T(2,128)} %table.1) | copy-start | bytes 79876
  2.9 0.7 %copy-start.2 = (s32[1,2,16,128]{3,2,1,0:T(8,128)S(1)}, s32[1,2,16,128]{3,2,1,0:T(8,128)}, u32[]{:S(2)}) copy-start(s32[1,2,16,128]{3,2,1,0:T(8,128)} %bins.1) | copy-start | bytes 49156
  3.6 6.6 %collective-permute-start.5 = (f32[1,4,2,16,128]{4,3,2,1,0:T(8,128)S(1)}, f32[1,4,2,16,128]{4,3,2,1,0:T(8,128)S(1)}, u32[]{:S(2)}, u32[]{:S(2)}) collective-permute-start(f32[1,4,2,16,128]{4,3,2,1,0:T(8,128)S(1)} %get-tuple-element.14), channel_id=1, source_target_pairs={{0,3},{1,2},{2,1},{3,0},{4,7},{5,6},{6,5},{7,4},{8,11},{9,10},{10,... | collective-permute-start | bytes 196616 | tf_op jit(solution)/shard_map/ppermute | solution.py:45
  5.0 3.4 %collective-permute-start.1 = (s32[2,2,16,128]{3,2,1,0:T(8,128)S(1)}, s32[2,2,16,128]{3,2,1,0:T(8,128)S(1)}, u32[]{:S(2)}, u32[]{:S(2)}) collective-permute-start(s32[2,2,16,128]{3,2,1,0:T(8,128)S(1)} %pad_add_fusion.3), channel_id=1, source_target_pairs={{0,9},{1,8},{2,11},{3,10},{4,13},{5,12},{6,15},{7,14},{8,1},{9,0},... | collective-permute-start | bytes 98312 | tf_op jit(solution)/shard_map/ppermute | solution.py:45
  8.4 4.0 %collective-permute-start.7 = (s32[2,2,16,128]{3,2,1,0:T(8,128)S(1)}, s32[2,2,16,128]{3,2,1,0:T(8,128)S(1)}, u32[]{:S(2)}, u32[]{:S(2)}) collective-permute-start(s32[2,2,16,128]{3,2,1,0:T(8,128)S(1)} %pad_add_fusion.2), channel_id=1, source_target_pairs={{0,5},{1,4},{2,7},{3,6},{4,1},{5,0},{6,3},{7,2},{8,13},{9,12},{10,... | collective-permute-start | bytes 98312 | tf_op jit(solution)/shard_map/ppermute | solution.py:45
  9.0 4.4 %collective-permute-start.2 = (s32[2,2,16,128]{3,2,1,0:T(8,128)S(1)}, s32[2,2,16,128]{3,2,1,0:T(8,128)S(1)}, u32[]{:S(2)}, u32[]{:S(2)}) collective-permute-start(s32[2,2,16,128]{3,2,1,0:T(8,128)S(1)} %pad_add_fusion.4), channel_id=1, source_target_pairs={{0,5},{1,4},{2,7},{3,6},{4,1},{5,0},{6,3},{7,2},{8,13},{9,12},{10,... | collective-permute-start | bytes 98312 | tf_op jit(solution)/shard_map/ppermute | solution.py:45
  10.2 8.4 %collective-permute-start.6 = (f32[2,4,2,16,128]{4,3,2,1,0:T(8,128)S(1)}, f32[2,4,2,16,128]{4,3,2,1,0:T(8,128)S(1)}, u32[]{:S(2)}, u32[]{:S(2)}) collective-permute-start(f32[2,4,2,16,128]{4,3,2,1,0:T(8,128)S(1)} %constant_dynamic-update-slice_fusion.surf_own), channel_id=1, source_target_pairs={{0,1},{1,0},{2,3},{3,2},{4,5},{5,4},{6,7},{7,6},{8,9},{9,8},{10,11... | collective-permute-start | bytes 393224 | tf_op jit(solution)/shard_map/ppermute | solution.py:45
  12.4 3.7 %collective-permute-start.8 = (s32[1,4,2,16,128]{4,3,2,1,0:T(8,128)S(1)}, s32[1,4,2,16,128]{4,3,2,1,0:T(8,128)S(1)}, u32[]{:S(2)}, u32[]{:S(2)}) collective-permute-start(s32[1,4,2,16,128]{4,3,2,1,0:T(8,128)S(1)} %add_bitcast_fusion.1), channel_id=1, source_target_pairs={{0,3},{1,2},{2,1},{3,0},{4,7},{5,6},{6,5},{7,4},{8,11},{9,10},{10,... | collective-permute-start | bytes 196616 | tf_op jit(solution)/shard_map/ppermute | solution.py:45
  13.3 4.7 %collective-permute-start.3 = (s32[1,4,2,16,128]{4,3,2,1,0:T(8,128)S(1)}, s32[1,4,2,16,128]{4,3,2,1,0:T(8,128)S(1)}, u32[]{:S(2)}, u32[]{:S(2)}) collective-permute-start(s32[1,4,2,16,128]{4,3,2,1,0:T(8,128)S(1)} %add_bitcast_fusion), channel_id=1, source_target_pairs={{0,3},{1,2},{2,1},{3,0},{4,7},{5,6},{6,5},{7,4},{8,11},{9,10},{10,... | collective-permute-start | bytes 196616 | tf_op jit(solution)/shard_map/ppermute | solution.py:45
  16.1 2.4 %collective-permute-start.9 = (s32[2,4,2,16,128]{4,3,2,1,0:T(8,128)S(1)}, s32[2,4,2,16,128]{4,3,2,1,0:T(8,128)S(1)}, u32[]{:S(2)}, u32[]{:S(2)}) collective-permute-start(s32[2,4,2,16,128]{4,3,2,1,0:T(8,128)S(1)} %pad_add_fusion.1.bins_own), channel_id=1, source_target_pairs={{0,1},{1,0},{2,3},{3,2},{4,5},{5,4},{6,7},{7,6},{8,9},{9,8},{10,11... | collective-permute-start | bytes 393224 | tf_op jit(solution)/shard_map/ppermute | solution.py:45
  18.1 4.0 %collective-permute-start.4 = (s32[2,4,2,16,128]{4,3,2,1,0:T(8,128)S(1)}, s32[2,4,2,16,128]{4,3,2,1,0:T(8,128)S(1)}, u32[]{:S(2)}, u32[]{:S(2)}) collective-permute-start(s32[2,4,2,16,128]{4,3,2,1,0:T(8,128)S(1)} %pad_add_fusion.bins_own), channel_id=1, source_target_pairs={{0,1},{1,0},{2,3},{3,2},{4,5},{5,4},{6,7},{7,6},{8,9},{9,8},{10,11... | collective-permute-start | bytes 393224 | tf_op jit(solution)/shard_map/ppermute | solution.py:45
  25.7 1.3 %collective-permute-start.10 = (f32[96,128]{1,0:T(8,128)S(1)}, f32[96,128]{1,0:T(8,128)S(1)}, u32[]{:S(2)}, u32[]{:S(2)}) collective-permute-start(f32[96,128]{1,0:T(8,128)S(1)} %get-tuple-element.16), channel_id=1, source_target_pairs={{0,1},{1,0},{2,3},{3,2},{4,5},{5,4},{6,7},{7,6},{8,9},{9,8},{10,11... | collective-permute-start | bytes 147464 | tf_op jit(solution)/shard_map/ppermute | solution.py:45

commit v4 on v3

--- a/solution.py
+++ b/solution.py
@@ -45,19 +45,8 @@
     return lax.ppermute(block, ("depth", "xline"), route)
 
 
-def stage_kernel(freqs, table, bins, surf, offsets, wide, bins_out, surf_out, offsets_out):
-    parity = lax.axis_index("xline") & 1
-    width = surf.shape[-1]
+def load_kernel(bins, bins_out):
     bins_out[...] = bins[...]
-    offsets_out[...] = offsets[...]
-    for kind in range(4):
-        block = surf[0, kind]
-        surf_out[0, kind] = -block if kind == 3 else block
-    for tap in range(len(TAP_ROWS)):
-        for part in range(2):
-            for freq in range(freqs):
-                row = table[tap, part, pl.ds(parity * freqs + freq, 1), :]
-                wide[(tap * 2 + part) * freqs + freq] = jnp.broadcast_to(row, (SUB, width))
 
 
 def clear_edges(buffer):
@@ -146,11 +135,30 @@
     lax.fori_loop(start, stop, slab_step, 0)
 
 
-def upper_kernel(sizes, wide, surf_own, surf_other, bins_own, bins_other, state, second):
+def upper_kernel(
+    sizes,
+    table,
+    offsets,
+    surf_own,
+    surf_other,
+    bins_own,
+    bins_other,
+    wide,
+    offsets_out,
+    state,
+    second,
+):
     depth_count, line_count, _, row_count, freqs, _ = sizes
     depth_index = lax.axis_index("depth")
     line_index = lax.axis_index("xline")
     near_count = line_count // 2
+    parity = line_index & 1
+    offsets_out[...] = offsets[...]
+    for tap in range(len(TAP_ROWS)):
+        for part in range(2):
+            for freq in range(freqs):
+                row = table[tap, part, pl.ds(parity * freqs + freq, 1), :]
+                wide[(tap * 2 + part) * freqs + freq] = jnp.broadcast_to(row, wide.shape[1:])
     clear_edges(state)
     clear_edges(second)
     for near in range(near_count):
@@ -160,7 +168,9 @@
             start = pl.multiple_of(PAD + line * row_count, SUB)
             for kind in range(4):
                 for freq in range(freqs):
-                    block = source[near, kind, (line_index & 1) * freqs + freq]
+                    block = source[near, kind, parity * freqs + freq]
+                    if kind == 3:
+                        block = -block
                     state[kind * freqs + freq, pl.ds(start, row_count), :] = block
     half = depth_count // 2
     stop = jnp.where(depth_index >= half, half, 0)
@@ -224,34 +234,21 @@
     f32 = jnp.float32
 
     def call(kernel, outs, scratch, flops, *args):
-        size = sum(array.size for array in (*args, *outs)) + sum(ref.shape[0] * ref.shape[1] * ref.shape[2] for ref in scratch)
+        size = sum(array.size for array in (*args, *outs, *scratch))
         return pl.pallas_call(
             kernel,
             out_shape=outs,
             in_specs=[VMEM] * len(args),
             out_specs=[VMEM] * len(outs),
-            scratch_shapes=scratch,
+            scratch_shapes=[pltpu.VMEM(array.shape, array.dtype) for array in scratch],
             compiler_params=pltpu.CompilerParams(vmem_limit_bytes=4 * size + (2 << 20)),
             cost_estimate=pl.CostEstimate(flops=flops, bytes_accessed=4 * size, transcendentals=0),
         )(*args)
 
+    like = jax.ShapeDtypeStruct
     surf = surface_fields.reshape(1, 4, 2 * freqs, row_count, width)
-    offsets = offset_list.T
-    like = jax.ShapeDtypeStruct
-    wide, bins, surf, offsets = call(
-        functools.partial(stage_kernel, freqs),
-        [
-            like((len(TAP_ROWS) * 2 * freqs, SUB, width), f32),
-            like(velocity_bins.shape, velocity_bins.dtype),
-            like(surf.shape, f32),
-            like(offsets.shape, offsets.dtype),
-        ],
-        [],
-        1000,
-        stencil_table,
-        velocity_bins,
-        surf,
-        offsets,
+    (bins,) = call(
+        load_kernel, [like(velocity_bins.shape, velocity_bins.dtype)], [], 1000, velocity_bins
     )
 
     far = hop(velocity_bins, depth_bits[0], 1)
@@ -273,14 +270,20 @@
     near_other = hop(near, 0, 1)
 
     field_shape = (4 * freqs, grid_rows + 2 * PAD, width)
-    field = pltpu.VMEM(field_shape, f32)
+    field = like(field_shape, f32)
     work = depth_count * levels * len(TAP_ROWS) * 8 * field_shape[0] * grid_rows * width
-    (state,) = call(
+    offsets = offset_list.T
+    wide, offsets, state = call(
         functools.partial(upper_kernel, sizes),
-        [like(field_shape, f32)],
+        [
+            like((len(TAP_ROWS) * 2 * freqs, SUB, width), f32),
+            like(offsets.shape, offsets.dtype),
+            field,
+        ],
         [field],
         work // 2,
-        wide,
+        stencil_table,
+        offsets,
         surf,
         surf_other,
         far,

time: 28.7 us -> 28.7 us (level)
  local copies, waits for them, and re-layouts: 2.99 us -> 0.77 us
  waiting for transfers between devices: 9.43 us -> 11.5 us
  starting transfers between devices: 7.37 us -> 7.73 us
    unnamed x9 -> x8, local copies, waits for them, and re-layouts: 2.98 us -> 0.77 us
    ppermute x11, waiting for transfers between devices: 9.43 us -> 11.5 us  [hop(): return lax.ppermute(block, ('depth', 'xline'), route)]
    ppermute x11, starting transfers between devices: 7.37 us -> 7.73 us  [hop(): return lax.ppermute(block, ('depth', 'xline'), route)]
  transfers between devices with their start and end apart: 11 -> 11, of which waited for: 6 -> 6; matrix products, arithmetic and copies ran while one was open for 0% -> 0% of each run, Pallas kernels for 13% -> 12%
where the time goes in v4:
time: 28.7 us; the launch traced here: 28.5 us
  waiting for transfers between devices  11.5 us (40%)
  Pallas kernels  8.38 us (29%)
  starting transfers between devices  7.73 us (27%)
  local copies, waits for them, and re-layouts  0.77 us (3%)
    ppermute x11, waiting for transfers between devices, hop(): return lax.ppermute(block, ('depth', 'xline'), route)  11.5 us
    ppermute x11, starting transfers between devices, hop(): return lax.ppermute(block, ('depth', 'xline'), route)  7.73 us
    pallas_call x3, Pallas kernels, call(): pl.pallas_call(kernel, out_shape=outs, in_specs=[VMEM] * len(args), out_s...  6.96 us
    pallas_call x1, Pallas kernels, shards(): pl.pallas_call(functools.partial(image_kernel, freqs), out_shape=like((1,...  1.41 us
    unnamed x8, local copies, waits for them, and re-layouts  0.77 us
  transfers between devices with their start and end apart: 11, of which 6 were waited for; matrix products, arithmetic and copies ran while one was open for 0% of the time, Pallas kernels for 12%

profile of v4, /device:TPU:29, one launch (start us, length us, event | category | flops | bytes accessed | tf_op | source)
XLA Modules:
  0.0 28.5 jit_solution(14600129204563673981)
XLA Ops:
  0.0 0.6 %collective-permute-start.2 = (s32[1,2,16,128]{3,2,1,0:T(8,128)}, s32[1,2,16,128]{3,2,1,0:T(8,128)S(1)}, u32[]{:S(2)}, u32[]{:S(2)}) collective-permute-start(s32[1,2,16,128]{3,2,1,0:T(8,128)} %bins.1), channel_id=1, source_target_pairs={{0,17},{1,16},{2,19},{3,18},{4,21},{5,20},{6,23},{7,22},{8,25},{9,... | collective-permute-start | bytes 49160 | tf_op jit(solution)/shard_map/ppermute | solution.py:45
  0.6 0.0 copy-start.1
  0.6 0.7 %copy-done.1 = s32[1,2,16,128]{3,2,1,0:T(8,128)S(1)} copy-done((s32[1,2,16,128]{3,2,1,0:T(8,128)S(1)}, s32[1,2,16,128]{3,2,1,0:T(8,128)}, u32[]{:S(2)}) %copy-start.1) | copy-done | bytes 16408
  1.4 0.0 copy-start.3
  1.4 3.6 %collective-permute-done.2 = s32[1,2,16,128]{3,2,1,0:T(8,128)S(1)} collective-permute-done((s32[1,2,16,128]{3,2,1,0:T(8,128)}, s32[1,2,16,128]{3,2,1,0:T(8,128)S(1)}, u32[]{:S(2)}, u32[]{:S(2)}) %collective-permute-start.2) | collective-permute-done | bytes 16416 | tf_op jit(solution)/shard_map/ppermute | solution.py:45
  5.0 0.2 collective-permute-start.3
  5.2 0.0 copy-done.3
  5.2 1.3 %collective-permute-start = (f32[1,4,2,16,128]{4,3,2,1,0:T(8,128)S(1)}, f32[1,4,2,16,128]{4,3,2,1,0:T(8,128)S(1)}, u32[]{:S(2)}, u32[]{:S(2)}) collective-permute-start(f32[1,4,2,16,128]{4,3,2,1,0:T(8,128)S(1)} %bitcast.7), channel_id=1, source_target_pairs={{0,3},{1,2},{2,1},{3,0},{4,7},{5,6},{6,5},{7,4},{8,11},{9,10},{10,... | collective-permute-start | bytes 196616 | tf_op jit(solution)/shard_map/ppermute | solution.py:45
  6.5 2.1 %collective-permute-done.3 = s32[2,2,16,128]{3,2,1,0:T(8,128)S(1)} collective-permute-done((s32[2,2,16,128]{3,2,1,0:T(8,128)S(1)}, s32[2,2,16,128]{3,2,1,0:T(8,128)S(1)}, u32[]{:S(2)}, u32[]{:S(2)}) %collective-permute-start.3) | collective-permute-done | bytes 32800 | tf_op jit(solution)/shard_map/ppermute | solution.py:45
  8.7 0.3 collective-permute-start.4
  9.0 1.5 %collective-permute-start.7 = (s32[2,2,16,128]{3,2,1,0:T(8,128)S(1)}, s32[2,2,16,128]{3,2,1,0:T(8,128)S(1)}, u32[]{:S(2)}, u32[]{:S(2)}) collective-permute-start(s32[2,2,16,128]{3,2,1,0:T(8,128)S(1)} %pad_add_fusion.4), channel_id=1, source_target_pairs={{0,5},{1,4},{2,7},{3,6},{4,1},{5,0},{6,3},{7,2},{8,13},{9,12},{10,... | collective-permute-start | bytes 98312 | tf_op jit(solution)/shard_map/ppermute | solution.py:45
  10.5 0.0 collective-permute-done
  10.5 0.2 collective-permute-start.1
  10.7 1.9 %collective-permute-done.4 = s32[2,2,16,128]{3,2,1,0:T(8,128)S(1)} collective-permute-done((s32[2,2,16,128]{3,2,1,0:T(8,128)S(1)}, s32[2,2,16,128]{3,2,1,0:T(8,128)S(1)}, u32[]{:S(2)}, u32[]{:S(2)}) %collective-permute-start.4) | collective-permute-done | bytes 32800 | tf_op jit(solution)/shard_map/ppermute | solution.py:45
  12.6 0.7 %collective-permute-start.5 = (s32[1,4,2,16,128]{4,3,2,1,0:T(8,128)S(1)}, s32[1,4,2,16,128]{4,3,2,1,0:T(8,128)S(1)}, u32[]{:S(2)}, u32[]{:S(2)}) collective-permute-start(s32[1,4,2,16,128]{4,3,2,1,0:T(8,128)S(1)} %add_bitcast_fusion), channel_id=1, source_target_pairs={{0,3},{1,2},{2,1},{3,0},{4,7},{5,6},{6,5},{7,4},{8,11},{9,10},{10,... | collective-permute-start | bytes 196616 | tf_op jit(solution)/shard_map/ppermute | solution.py:45
  13.3 0.0 collective-permute-done.7
  13.3 1.1 %collective-permute-start.8 = (s32[1,4,2,16,128]{4,3,2,1,0:T(8,128)S(1)}, s32[1,4,2,16,128]{4,3,2,1,0:T(8,128)S(1)}, u32[]{:S(2)}, u32[]{:S(2)}) collective-permute-start(s32[1,4,2,16,128]{4,3,2,1,0:T(8,128)S(1)} %add_bitcast_fusion.1), channel_id=1, source_target_pairs={{0,3},{1,2},{2,1},{3,0},{4,7},{5,6},{6,5},{7,4},{8,11},{9,10},{10,... | collective-permute-start | bytes 196616 | tf_op jit(solution)/shard_map/ppermute | solution.py:45
  14.4 1.9 %collective-permute-done.5 = s32[1,4,2,16,128]{4,3,2,1,0:T(8,128)S(1)} collective-permute-done((s32[1,4,2,16,128]{4,3,2,1,0:T(8,128)S(1)}, s32[1,4,2,16,128]{4,3,2,1,0:T(8,128)S(1)}, u32[]{:S(2)}, u32[]{:S(2)}) %collective-permute-start.5) | collective-permute-done | bytes 65568 | tf_op jit(solution)/shard_map/ppermute | solution.py:45
  16.3 0.0 copy-start
  16.3 0.4 %collective-permute-start.6 = (s32[2,4,2,16,128]{4,3,2,1,0:T(8,128)S(1)}, s32[2,4,2,16,128]{4,3,2,1,0:T(8,128)S(1)}, u32[]{:S(2)}, u32[]{:S(2)}) collective-permute-start(s32[2,4,2,16,128]{4,3,2,1,0:T(8,128)S(1)} %pad_add_fusion.bins_own), channel_id=1, source_target_pairs={{0,1},{1,0},{2,3},{3,2},{4,5},{5,4},{6,7},{7,6},{8,9},{9,8},{10,11... | collective-permute-start | bytes 393224 | tf_op jit(solution)/shard_map/ppermute | solution.py:45
  16.7 1.1 %collective-permute-done.8 = s32[1,4,2,16,128]{4,3,2,1,0:T(8,128)S(1)} collective-permute-done((s32[1,4,2,16,128]{4,3,2,1,0:T(8,128)S(1)}, s32[1,4,2,16,128]{4,3,2,1,0:T(8,128)S(1)}, u32[]{:S(2)}, u32[]{:S(2)}) %collective-permute-start.8) | collective-permute-done | bytes 65568 | tf_op jit(solution)/shard_map/ppermute | solution.py:45
  17.8 0.0 copy-start.2
  17.8 0.7 %collective-permute-start.9 = (s32[2,4,2,16,128]{4,3,2,1,0:T(8,128)S(1)}, s32[2,4,2,16,128]{4,3,2,1,0:T(8,128)S(1)}, u32[]{:S(2)}, u32[]{:S(2)}) collective-permute-start(s32[2,4,2,16,128]{4,3,2,1,0:T(8,128)S(1)} %pad_add_fusion.1.bins_own), channel_id=1, source_target_pairs={{0,1},{1,0},{2,3},{3,2},{4,5},{5,4},{6,7},{7,6},{8,9},{9,8},{10,11... | collective-permute-start | bytes 393224 | tf_op jit(solution)/shard_map/ppermute | solution.py:45
  18.5 0.0 collective-permute-done.1.surf_other
  18.5 0.0 collective-permute-done.6.bins_other
  18.5 0.0 copy-done
  18.5 0.0 copy-done.2
  18.6 3.5 %shard_map.47 = (f32[26,8,128]{2,1,0:T(8,128)S(1)}, s32[2,16]{1,0:T(2,128)S(1)}, f32[4,80,128]{2,1,0:T(8,128)S(1)}) custom-call(f32[13,2,2,128]{3,2,1,0:T(2,128)S(1)} %copy-done, s32[2,16]{1,0:T(2,128)S(1)} %bitcast.6, f32[2,4,2,16,128]{4,3,2,1,0:T(8,128)S(1)} %pad_maximum_fusion.surf_own, f32[2,4,2,16,128]{4,3,2,1,0:T(8,128)S(1)} %collective-permute-done.1.surf_other, ...), custom_call_target="tpu_custom_call" | custom-call | flops 27262976 | bytes 985344 | tf_op jit(solution)/shard_map/pallas_call | solution.py:238
  22.0 0.0 collective-permute-done.9.bins_other
  22.1 3.5 %shard_map.48 = (f32[96,128]{1,0:T(8,128)S(1)}, f32[96,128]{1,0:T(8,128)S(1)}) custom-call(f32[26,8,128]{2,1,0:T(8,128)S(1)} %get-tuple-element.11.wide, s32[2,4,2,16,128]{4,3,2,1,0:T(8,128)S(1)} %pad_add_fusion.1.bins_own, s32[2,4,2,16,128]{4,3,2,1,0:T(8,128)S(1)} %collective-permute-done.9.bins_other, f32[4,80,128]{2,1,0:T(8,128)S(1)} %get-tuple-element.12.state), custom_call_target="tpu_custom_call" | custom-call | flops 27262976 | bytes 958464 | tf_op jit(solution)/shard_map/pallas_call | solution.py:238
  25.5 0.6 %collective-permute-start.10 = (f32[96,128]{1,0:T(8,128)S(1)}, f32[96,128]{1,0:T(8,128)S(1)}, u32[]{:S(2)}, u32[]{:S(2)}) collective-permute-start(f32[96,128]{1,0:T(8,128)S(1)} %get-tuple-element.14), channel_id=1, source_target_pairs={{0,1},{1,0},{2,3},{3,2},{4,5},{5,4},{6,7},{7,6},{8,9},{9,8},{10,11... | collective-permute-start | bytes 147464 | tf_op jit(solution)/shard_map/ppermute | solution.py:45
  26.2 0.9 %collective-permute-done.10.other = f32[96,128]{1,0:T(8,128)S(1)} collective-permute-done((f32[96,128]{1,0:T(8,128)S(1)}, f32[96,128]{1,0:T(8,128)S(1)}, u32[]{:S(2)}, u32[]{:S(2)}) %collective-permute-start.10) | collective-permute-done | bytes 49184 | tf_op jit(solution)/shard_map/ppermute | solution.py:45
  27.1 1.4 %imaging.1 = f32[1,16,16,128]{3,2,1,0:T(8,128)} custom-call(s32[2,16]{1,0:T(2,128)S(1)} %get-tuple-element.10.offsets, f32[96,128]{1,0:T(8,128)S(1)} %get-tuple-element.13.mine, f32[96,128]{1,0:T(8,128)S(1)} %collective-permute-done.10.other), custom_call_target="tpu_custom_call" | custom-call | tf_op jit(solution)/shard_map/imaging/pallas_call | solution.py:304
  (10 shorter events, 0.1 us)
Async XLA Ops:
  0.0 5.0 %collective-permute-start.2 = (s32[1,2,16,128]{3,2,1,0:T(8,128)}, s32[1,2,16,128]{3,2,1,0:T(8,128)S(1)}, u32[]{:S(2)}, u32[]{:S(2)}) collective-permute-start(s32[1,2,16,128]{3,2,1,0:T(8,128)} %bins.1), channel_id=1, source_target_pairs={{0,17},{1,16},{2,19},{3,18},{4,21},{5,20},{6,23},{7,22},{8,25},{9,... | collective-permute-start | bytes 49160 | tf_op jit(solution)/shard_map/ppermute | solution.py:45
  0.6 0.8 %copy-start.1 = (s32[1,2,16,128]{3,2,1,0:T(8,128)S(1)}, s32[1,2,16,128]{3,2,1,0:T(8,128)}, u32[]{:S(2)}) copy-start(s32[1,2,16,128]{3,2,1,0:T(8,128)} %bins.1) | copy-start | bytes 49156
  1.4 3.8 %copy-start.3 = (f32[2,2,2,16,128]{4,3,2,1,0:T(8,128)S(1)}, f32[2,2,2,16,128]{4,3,2,1,0:T(8,128)}, u32[]{:S(2)}) copy-start(f32[2,2,2,16,128]{4,3,2,1,0:T(8,128)} %param.4) | copy-start | bytes 196612
  5.0 3.7 %collective-permute-start.3 = (s32[2,2,16,128]{3,2,1,0:T(8,128)S(1)}, s32[2,2,16,128]{3,2,1,0:T(8,128)S(1)}, u32[]{:S(2)}, u32[]{:S(2)}) collective-permute-start(s32[2,2,16,128]{3,2,1,0:T(8,128)S(1)} %pad_add_fusion.3), channel_id=1, source_target_pairs={{0,9},{1,8},{2,11},{3,10},{4,13},{5,12},{6,15},{7,14},{8,1},{9,0},... | collective-permute-start | bytes 98312 | tf_op jit(solution)/shard_map/ppermute | solution.py:45
  5.2 5.3 %collective-permute-start = (f32[1,4,2,16,128]{4,3,2,1,0:T(8,128)S(1)}, f32[1,4,2,16,128]{4,3,2,1,0:T(8,128)S(1)}, u32[]{:S(2)}, u32[]{:S(2)}) collective-permute-start(f32[1,4,2,16,128]{4,3,2,1,0:T(8,128)S(1)} %bitcast.7), channel_id=1, source_target_pairs={{0,3},{1,2},{2,1},{3,0},{4,7},{5,6},{6,5},{7,4},{8,11},{9,10},{10,... | collective-permute-start | bytes 196616 | tf_op jit(solution)/shard_map/ppermute | solution.py:45
  8.7 3.9 %collective-permute-start.4 = (s32[2,2,16,128]{3,2,1,0:T(8,128)S(1)}, s32[2,2,16,128]{3,2,1,0:T(8,128)S(1)}, u32[]{:S(2)}, u32[]{:S(2)}) collective-permute-start(s32[2,2,16,128]{3,2,1,0:T(8,128)S(1)} %pad_add_fusion.2), channel_id=1, source_target_pairs={{0,5},{1,4},{2,7},{3,6},{4,1},{5,0},{6,3},{7,2},{8,13},{9,12},{10,... | collective-permute-start | bytes 98312 | tf_op jit(solution)/shard_map/ppermute | solution.py:45
  9.0 4.3 %collective-permute-start.7 = (s32[2,2,16,128]{3,2,1,0:T(8,128)S(1)}, s32[2,2,16,128]{3,2,1,0:T(8,128)S(1)}, u32[]{:S(2)}, u32[]{:S(2)}) collective-permute-start(s32[2,2,16,128]{3,2,1,0:T(8,128)S(1)} %pad_add_fusion.4), channel_id=1, source_target_pairs={{0,5},{1,4},{2,7},{3,6},{4,1},{5,0},{6,3},{7,2},{8,13},{9,12},{10,... | collective-permute-start | bytes 98312 | tf_op jit(solution)/shard_map/ppermute | solution.py:45
  10.5 8.0 %collective-permute-start.1 = (f32[2,4,2,16,128]{4,3,2,1,0:T(8,128)S(1)}, f32[2,4,2,16,128]{4,3,2,1,0:T(8,128)S(1)}, u32[]{:S(2)}, u32[]{:S(2)}) collective-permute-start(f32[2,4,2,16,128]{4,3,2,1,0:T(8,128)S(1)} %pad_maximum_fusion.surf_own), channel_id=1, source_target_pairs={{0,1},{1,0},{2,3},{3,2},{4,5},{5,4},{6,7},{7,6},{8,9},{9,8},{10,11... | collective-permute-start | bytes 393224 | tf_op jit(solution)/shard_map/ppermute | solution.py:45
  12.6 3.7 %collective-permute-start.5 = (s32[1,4,2,16,128]{4,3,2,1,0:T(8,128)S(1)}, s32[1,4,2,16,128]{4,3,2,1,0:T(8,128)S(1)}, u32[]{:S(2)}, u32[]{:S(2)}) collective-permute-start(s32[1,4,2,16,128]{4,3,2,1,0:T(8,128)S(1)} %add_bitcast_fusion), channel_id=1, source_target_pairs={{0,3},{1,2},{2,1},{3,0},{4,7},{5,6},{6,5},{7,4},{8,11},{9,10},{10,... | collective-permute-start | bytes 196616 | tf_op jit(solution)/shard_map/ppermute | solution.py:45
  13.3 4.5 %collective-permute-start.8 = (s32[1,4,2,16,128]{4,3,2,1,0:T(8,128)S(1)}, s32[1,4,2,16,128]{4,3,2,1,0:T(8,128)S(1)}, u32[]{:S(2)}, u32[]{:S(2)}) collective-permute-start(s32[1,4,2,16,128]{4,3,2,1,0:T(8,128)S(1)} %add_bitcast_fusion.1), channel_id=1, source_target_pairs={{0,3},{1,2},{2,1},{3,0},{4,7},{5,6},{6,5},{7,4},{8,11},{9,10},{10,... | collective-permute-start | bytes 196616 | tf_op jit(solution)/shard_map/ppermute | solution.py:45
  16.3 2.2 %copy-start = (f32[13,2,2,128]{3,2,1,0:T(2,128)S(1)}, f32[13,2,2,128]{3,2,1,0:T(2,128)}, u32[]{:S(2)}) copy-start(f32[13,2,2,128]{3,2,1,0:T(2,128)} %table.1) | copy-start | bytes 79876
  16.3 2.2 %collective-permute-start.6 = (s32[2,4,2,16,128]{4,3,2,1,0:T(8,128)S(1)}, s32[2,4,2,16,128]{4,3,2,1,0:T(8,128)S(1)}, u32[]{:S(2)}, u32[]{:S(2)}) collective-permute-start(s32[2,4,2,16,128]{4,3,2,1,0:T(8,128)S(1)} %pad_add_fusion.bins_own), channel_id=1, source_target_pairs={{0,1},{1,0},{2,3},{3,2},{4,5},{5,4},{6,7},{7,6},{8,9},{9,8},{10,11... | collective-permute-start | bytes 393224 | tf_op jit(solution)/shard_map/ppermute | solution.py:45
  17.8 0.7 %copy-start.2 = (s32[16,2]{0,1:T(2,128)S(1)}, s32[16,2]{0,1:T(2,128)}, u32[]{:S(2)}) copy-start(s32[16,2]{0,1:T(2,128)} %param.7) | copy-start | bytes 388
  17.8 4.2 %collective-permute-start.9 = (s32[2,4,2,16,128]{4,3,2,1,0:T(8,128)S(1)}, s32[2,4,2,16,128]{4,3,2,1,0:T(8,128)S(1)}, u32[]{:S(2)}, u32[]{:S(2)}) collective-permute-start(s32[2,4,2,16,128]{4,3,2,1,0:T(8,128)S(1)} %pad_add_fusion.1.bins_own), channel_id=1, source_target_pairs={{0,1},{1,0},{2,3},{3,2},{4,5},{5,4},{6,7},{7,6},{8,9},{9,8},{10,11... | collective-permute-start | bytes 393224 | tf_op jit(solution)/shard_map/ppermute | solution.py:45
  25.5 1.5 %collective-permute-start.10 = (f32[96,128]{1,0:T(8,128)S(1)}, f32[96,128]{1,0:T(8,128)S(1)}, u32[]{:S(2)}, u32[]{:S(2)}) collective-permute-start(f32[96,128]{1,0:T(8,128)S(1)} %get-tuple-element.14), channel_id=1, source_target_pairs={{0,1},{1,0},{2,3},{3,2},{4,5},{5,4},{6,7},{7,6},{8,9},{9,8},{10,11... | collective-permute-start | bytes 147464 | tf_op jit(solution)/shard_map/ppermute | solution.py:45

commit v5 on v4

--- a/solution.py
+++ b/solution.py
@@ -135,7 +135,13 @@
     lax.fori_loop(start, stop, slab_step, 0)
 
 
-def upper_kernel(
+def far_slabs(depth_count, first_part):
+    half = depth_count // 2
+    count = jnp.where(lax.axis_index("depth") >= half, half, 0)
+    return (0, count // 2) if first_part else (count // 2, count)
+
+
+def begin_kernel(
     sizes,
     table,
     offsets,
@@ -149,7 +155,6 @@
     second,
 ):
     depth_count, line_count, _, row_count, freqs, _ = sizes
-    depth_index = lax.axis_index("depth")
     line_index = lax.axis_index("xline")
     near_count = line_count // 2
     parity = line_index & 1
@@ -172,19 +177,22 @@
                     if kind == 3:
                         block = -block
                     state[kind * freqs + freq, pl.ds(start, row_count), :] = block
-    half = depth_count // 2
-    stop = jnp.where(depth_index >= half, half, 0)
-    run_slabs(sizes, 0, stop, wide, bins_own, bins_other, state, second)
-
-
-def lower_kernel(sizes, wide, bins_own, bins_other, state, mine, theirs, first, second):
+    run_slabs(sizes, *far_slabs(depth_count, True), wide, bins_own, bins_other, state, second)
+
+
+def middle_kernel(sizes, wide, bins_own, bins_other, before, state, second):
+    state[...] = before[...]
+    clear_edges(second)
+    run_slabs(sizes, *far_slabs(sizes[0], False), wide, bins_own, bins_other, state, second)
+
+
+def finish_kernel(sizes, wide, bins_own, bins_other, before, mine, theirs, first, second):
     depth_count, _, _, row_count, freqs, _ = sizes
     depth_index = lax.axis_index("depth")
     line_index = lax.axis_index("xline")
-    first[...] = state[...]
+    first[...] = before[...]
     clear_edges(second)
-    half = depth_count // 2
-    start = jnp.where(depth_index >= half, half, 0)
+    start = jnp.where(depth_index >= depth_count // 2, depth_count // 2, 0)
     run_slabs(sizes, start, depth_index + 1, wide, bins_own, bins_other, first, second)
     tall = row_count + 2 * OFF_Y
     for out, line in ((mine, line_index), (theirs, line_index ^ 1)):
@@ -251,37 +259,54 @@
         load_kernel, [like(velocity_bins.shape, velocity_bins.dtype)], [], 1000, velocity_bins
     )
 
-    far = hop(velocity_bins, depth_bits[0], 1)
-    near = bins
-    for bit in line_bits:
+    top, below = depth_bits[:2]
+    last, line = depth_bits[-1], line_bits[0]
+    from_top, from_both, from_below = [
+        hop(velocity_bins, bit, bit.bit_count() & 1)
+        for bit in (top, top | below, below)
+    ]
+    far = jnp.concatenate([from_top, from_both], axis=0)
+    near = jnp.concatenate([bins, from_below], axis=0)
+    surf = jnp.concatenate([surf, hop(surf, 0, line | 1)], axis=0)
+    for bit in depth_bits[2:-1]:
+        part = hop(jnp.concatenate([far, near], axis=0), bit, 1)
+        far = jnp.concatenate([far, part[: far.shape[0]]], axis=0)
+        near = jnp.concatenate([near, part[near.shape[0] :]], axis=0)
+    part = hop(jnp.concatenate([far, near], axis=0), last, 1)
+    count = far.shape[0]
+
+    def along_line(bins, deeper):
+        line_part = hop(bins, 0, line | 1)
+        cross_part = hop(bins, last, line)
+        bins = jnp.stack(
+            [
+                jnp.concatenate([bins, deeper], axis=0),
+                jnp.concatenate([line_part, cross_part], axis=0),
+            ]
+        )
+        for bit in line_bits[1:]:
+            bins = jnp.concatenate([bins, hop(bins, 0, bit | 1)], axis=0)
+        return bins, hop(bins, 0, 1)
+
+    far, far_other = along_line(far, part[:count])
+    near, near_other = along_line(near, part[count:])
+    for bit in line_bits[1:]:
         surf = jnp.concatenate([surf, hop(surf, 0, bit | 1)], axis=0)
-    for bit in depth_bits[1:-1]:
-        both = hop(jnp.concatenate([far, near], axis=0), bit, 1)
-        count = far.shape[0]
-        far = jnp.concatenate([far, both[:count]], axis=0)
-        near = jnp.concatenate([near, both[count:]], axis=0)
     surf_other = hop(surf, 0, 1)
-    far = jnp.concatenate([far, hop(far, depth_bits[-1], 1)], axis=0)[None]
-    near = jnp.concatenate([near, hop(near, depth_bits[-1], 1)], axis=0)[None]
-    for bit in line_bits:
-        far = jnp.concatenate([far, hop(far, 0, bit | 1)], axis=0)
-        near = jnp.concatenate([near, hop(near, 0, bit | 1)], axis=0)
-    far_other = hop(far, 0, 1)
-    near_other = hop(near, 0, 1)
 
     field_shape = (4 * freqs, grid_rows + 2 * PAD, width)
     field = like(field_shape, f32)
     work = depth_count * levels * len(TAP_ROWS) * 8 * field_shape[0] * grid_rows * width
     offsets = offset_list.T
     wide, offsets, state = call(
-        functools.partial(upper_kernel, sizes),
+        functools.partial(begin_kernel, sizes),
         [
             like((len(TAP_ROWS) * 2 * freqs, SUB, width), f32),
             like(offsets.shape, offsets.dtype),
             field,
         ],
         [field],
-        work // 2,
+        work // 4,
         stencil_table,
         offsets,
         surf,
@@ -289,9 +314,19 @@
         far,
         far_other,
     )
+    (state,) = call(
+        functools.partial(middle_kernel, sizes),
+        [field],
+        [field],
+        work // 4,
+        wide,
+        far,
+        far_other,
+        state,
+    )
     pack = like((2 * freqs * (2 * row_count + 2 * OFF_Y), width), f32)
     mine, theirs = call(
-        functools.partial(lower_kernel, sizes),
+        functools.partial(finish_kernel, sizes),
         [pack, pack],
         [field, field],
         work // 2,

time: 28.7 us -> 26.1 us (0.909)
  the two profiles are of different devices: /device:TPU:29 before, /device:TPU:31 now
where the time goes in v5:
time: 26.1 us; the launch traced here: 25.9 us
  starting transfers between devices  10.8 us (41%)
  Pallas kernels  8.42 us (32%)
  waiting for transfers between devices  5.76 us (22%)
  local copies, waits for them, and re-layouts  0.74 us (3%)
    ppermute x13, starting transfers between devices, hop(): return lax.ppermute(block, ('depth', 'xline'), route)  10.8 us
    pallas_call x4, Pallas kernels, call(): pl.pallas_call(kernel, out_shape=outs, in_specs=[VMEM] * len(args), out_s...  7 us
    ppermute x13, waiting for transfers between devices, hop(): return lax.ppermute(block, ('depth', 'xline'), route)  5.76 us
    pallas_call x1, Pallas kernels, shards(): pl.pallas_call(functools.partial(image_kernel, freqs), out_shape=like((1,...  1.41 us
    unnamed x9, local copies, waits for them, and re-layouts  0.74 us
  transfers between devices with their start and end apart: 13, of which 7 were waited for; matrix products, arithmetic and copies ran while one was open for 0% of the time, Pallas kernels for 14%

profile of v5, /device:TPU:31, one launch (start us, length us, event | category | flops | bytes accessed | tf_op | source)
XLA Modules:
  0.0 25.9 jit_solution(4204240323624094227)
XLA Ops:
  0.0 0.6 %collective-permute-start.2 = (s32[1,2,16,128]{3,2,1,0:T(8,128)}, s32[1,2,16,128]{3,2,1,0:T(8,128)S(1)}, u32[]{:S(2)}, u32[]{:S(2)}) collective-permute-start(s32[1,2,16,128]{3,2,1,0:T(8,128)} %bins.1), channel_id=1, source_target_pairs={{0,17},{1,16},{2,19},{3,18},{4,21},{5,20},{6,23},{7,22},{8,25},{9,... | collective-permute-start | bytes 49160 | tf_op jit(solution)/shard_map/ppermute | solution.py:45
  0.6 2.2 %collective-permute-start.3 = (s32[1,2,16,128]{3,2,1,0:T(8,128)}, s32[1,2,16,128]{3,2,1,0:T(8,128)S(1)}, u32[]{:S(2)}, u32[]{:S(2)}) collective-permute-start(s32[1,2,16,128]{3,2,1,0:T(8,128)} %bins.1), channel_id=1, source_target_pairs={{0,24},{1,25},{2,26},{3,27},{4,28},{5,29},{6,30},{7,31},{8,16},{9,... | collective-permute-start | bytes 49160 | tf_op jit(solution)/shard_map/ppermute | solution.py:45
  2.8 0.4 %collective-permute-start.4 = (s32[1,2,16,128]{3,2,1,0:T(8,128)}, s32[1,2,16,128]{3,2,1,0:T(8,128)S(1)}, u32[]{:S(2)}, u32[]{:S(2)}) collective-permute-start(s32[1,2,16,128]{3,2,1,0:T(8,128)} %bins.1), channel_id=1, source_target_pairs={{0,9},{1,8},{2,11},{3,10},{4,13},{5,12},{6,15},{7,14},{8,1},{9,0},... | collective-permute-start | bytes 49160 | tf_op jit(solution)/shard_map/ppermute | solution.py:45
  3.2 0.5 %collective-permute-start = (f32[1,4,2,16,128]{4,3,2,1,0:T(8,128)}, f32[1,4,2,16,128]{4,3,2,1,0:T(8,128)S(1)}, u32[]{:S(2)}, u32[]{:S(2)}) collective-permute-start(f32[1,4,2,16,128]{4,3,2,1,0:T(8,128)} %bitcast.11), channel_id=1, source_target_pairs={{0,3},{1,2},{2,1},{3,0},{4,7},{5,6},{6,5},{7,4},{8,11},{9,10},{10,... | collective-permute-start | bytes 196616 | tf_op jit(solution)/shard_map/ppermute | solution.py:45
  3.7 0.0 copy-start.1
  3.7 0.7 %copy-done.1 = s32[1,2,16,128]{3,2,1,0:T(8,128)S(1)} copy-done((s32[1,2,16,128]{3,2,1,0:T(8,128)S(1)}, s32[1,2,16,128]{3,2,1,0:T(8,128)}, u32[]{:S(2)}) %copy-start.1) | copy-done | bytes 16408
  4.5 0.5 %collective-permute-done.2 = s32[1,2,16,128]{3,2,1,0:T(8,128)S(1)} collective-permute-done((s32[1,2,16,128]{3,2,1,0:T(8,128)}, s32[1,2,16,128]{3,2,1,0:T(8,128)S(1)}, u32[]{:S(2)}, u32[]{:S(2)}) %collective-permute-start.2) | collective-permute-done | bytes 16416 | tf_op jit(solution)/shard_map/ppermute | solution.py:45
  5.0 0.2 collective-permute-done.3
  5.2 1.4 %collective-permute-start.6 = (s32[2,2,16,128]{3,2,1,0:T(8,128)S(1)}, s32[2,2,16,128]{3,2,1,0:T(8,128)S(1)}, u32[]{:S(2)}, u32[]{:S(2)}) collective-permute-start(s32[2,2,16,128]{3,2,1,0:T(8,128)S(1)} %constant_dynamic-update-slice_fusion), channel_id=1, source_target_pairs={{0,3},{1,2},{2,1},{3,0},{4,7},{5,6},{6,5},{7,4},{8,11},{9,10},{10,... | collective-permute-start | bytes 98312 | tf_op jit(solution)/shard_map/ppermute | solution.py:45
  6.6 1.2 %collective-permute-start.7 = (s32[2,2,16,128]{3,2,1,0:T(8,128)S(1)}, s32[2,2,16,128]{3,2,1,0:T(8,128)S(1)}, u32[]{:S(2)}, u32[]{:S(2)}) collective-permute-start(s32[2,2,16,128]{3,2,1,0:T(8,128)S(1)} %constant_dynamic-update-slice_fusion), channel_id=1, source_target_pairs={{0,6},{1,7},{2,4},{3,5},{4,2},{5,3},{6,0},{7,1},{8,14},{9,15},{10,... | collective-permute-start | bytes 98312 | tf_op jit(solution)/shard_map/ppermute | solution.py:45
  7.8 0.0 collective-permute-done.4
  7.8 1.2 %collective-permute-start.10 = (s32[2,2,16,128]{3,2,1,0:T(8,128)S(1)}, s32[2,2,16,128]{3,2,1,0:T(8,128)S(1)}, u32[]{:S(2)}, u32[]{:S(2)}) collective-permute-start(s32[2,2,16,128]{3,2,1,0:T(8,128)S(1)} %pad_add_fusion.4), channel_id=1, source_target_pairs={{0,6},{1,7},{2,4},{3,5},{4,2},{5,3},{6,0},{7,1},{8,14},{9,15},{10,... | collective-permute-start | bytes 98312 | tf_op jit(solution)/shard_map/ppermute | solution.py:45
  9.0 0.9 %collective-permute-start.9 = (s32[2,2,16,128]{3,2,1,0:T(8,128)S(1)}, s32[2,2,16,128]{3,2,1,0:T(8,128)S(1)}, u32[]{:S(2)}, u32[]{:S(2)}) collective-permute-start(s32[2,2,16,128]{3,2,1,0:T(8,128)S(1)} %pad_add_fusion.4), channel_id=1, source_target_pairs={{0,3},{1,2},{2,1},{3,0},{4,7},{5,6},{6,5},{7,4},{8,11},{9,10},{10,... | collective-permute-start | bytes 98312 | tf_op jit(solution)/shard_map/ppermute | solution.py:45
  9.9 0.0 collective-permute-done.6
  9.9 0.9 %collective-permute-start.5 = (s32[4,2,16,128]{3,2,1,0:T(8,128)S(1)}, s32[4,2,16,128]{3,2,1,0:T(8,128)S(1)}, u32[]{:S(2)}, u32[]{:S(2)}) collective-permute-start(s32[4,2,16,128]{3,2,1,0:T(8,128)S(1)} %pad_add_fusion.2), channel_id=1, source_target_pairs={{0,5},{1,4},{2,7},{3,6},{4,1},{5,0},{6,3},{7,2},{8,13},{9,12},{10,... | collective-permute-start | bytes 196616 | tf_op jit(solution)/shard_map/ppermute | solution.py:45
  10.8 0.0 collective-permute-done.7
  10.8 0.0 copy-start.3
  10.8 1.2 %collective-permute-done.10 = s32[2,2,16,128]{3,2,1,0:T(8,128)S(1)} collective-permute-done((s32[2,2,16,128]{3,2,1,0:T(8,128)S(1)}, s32[2,2,16,128]{3,2,1,0:T(8,128)S(1)}, u32[]{:S(2)}, u32[]{:S(2)}) %collective-permute-start.10) | collective-permute-done | bytes 32800 | tf_op jit(solution)/shard_map/ppermute | solution.py:45
  12.1 0.6 %collective-permute-done.9 = s32[2,2,16,128]{3,2,1,0:T(8,128)S(1)} collective-permute-done((s32[2,2,16,128]{3,2,1,0:T(8,128)S(1)}, s32[2,2,16,128]{3,2,1,0:T(8,128)S(1)}, u32[]{:S(2)}, u32[]{:S(2)}) %collective-permute-start.9) | collective-permute-done | bytes 32800 | tf_op jit(solution)/shard_map/ppermute | solution.py:45
  12.7 0.0 collective-permute-done
  12.7 0.0 copy-done.3
  12.7 0.5 %collective-permute-start.1 = (f32[2,4,2,16,128]{4,3,2,1,0:T(8,128)S(1)}, f32[2,4,2,16,128]{4,3,2,1,0:T(8,128)S(1)}, u32[]{:S(2)}, u32[]{:S(2)}) collective-permute-start(f32[2,4,2,16,128]{4,3,2,1,0:T(8,128)S(1)} %pad_maximum_fusion.surf_own), channel_id=1, source_target_pairs={{0,1},{1,0},{2,3},{3,2},{4,5},{5,4},{6,7},{7,6},{8,9},{9,8},{10,11... | collective-permute-start | bytes 393224 | tf_op jit(solution)/shard_map/ppermute | solution.py:45
  13.2 1.4 %collective-permute-done.5 = s32[4,2,16,128]{3,2,1,0:T(8,128)S(1)} collective-permute-done((s32[4,2,16,128]{3,2,1,0:T(8,128)S(1)}, s32[4,2,16,128]{3,2,1,0:T(8,128)S(1)}, u32[]{:S(2)}, u32[]{:S(2)}) %collective-permute-start.5) | collective-permute-done | bytes 65568 | tf_op jit(solution)/shard_map/ppermute | solution.py:45
  14.7 0.5 %collective-permute-start.8 = (s32[2,4,2,16,128]{4,3,2,1,0:T(8,128)S(1)}, s32[2,4,2,16,128]{4,3,2,1,0:T(8,128)S(1)}, u32[]{:S(2)}, u32[]{:S(2)}) collective-permute-start(s32[2,4,2,16,128]{4,3,2,1,0:T(8,128)S(1)} %pad_add_fusion.bins_own), channel_id=1, source_target_pairs={{0,1},{1,0},{2,3},{3,2},{4,5},{5,4},{6,7},{7,6},{8,9},{9,8},{10,11... | collective-permute-start | bytes 393224 | tf_op jit(solution)/shard_map/ppermute | solution.py:45
  15.2 0.0 copy-start
  15.2 0.0 copy-start.2
  15.2 0.2 collective-permute-start.11
  15.4 0.0 collective-permute-done.1.surf_other
  15.4 0.8 %collective-permute-done.8.bins_other = s32[2,4,2,16,128]{4,3,2,1,0:T(8,128)S(1)} collective-permute-done((s32[2,4,2,16,128]{4,3,2,1,0:T(8,128)S(1)}, s32[2,4,2,16,128]{4,3,2,1,0:T(8,128)S(1)}, u32[]{:S(2)}, u32[]{:S(2)}) %collective-permute-start.8) | collective-permute-done | bytes 131104 | tf_op jit(solution)/shard_map/ppermute | solution.py:45
  16.1 0.0 copy-done
  16.1 0.0 copy-done.2
  16.1 1.8 %shard_map.47 = (f32[26,8,128]{2,1,0:T(8,128)S(1)}, s32[2,16]{1,0:T(2,128)S(1)}, f32[4,80,128]{2,1,0:T(8,128)S(1)}) custom-call(f32[13,2,2,128]{3,2,1,0:T(2,128)S(1)} %copy-done, s32[2,16]{1,0:T(2,128)S(1)} %bitcast.10, f32[2,4,2,16,128]{4,3,2,1,0:T(8,128)S(1)} %pad_maximum_fusion.surf_own, f32[2,4,2,16,128]{4,3,2,1,0:T(8,128)S(1)} %collective-permute-done.1.surf_other, ...), custom_call_target="tpu_custom_call" | custom-call | flops 13631488 | bytes 985344 | tf_op jit(solution)/shard_map/pallas_call | solution.py:246
  17.9 1.7 %shard_map.48.before = f32[4,80,128]{2,1,0:T(8,128)S(1)} custom-call(f32[26,8,128]{2,1,0:T(8,128)S(1)} %get-tuple-element.11.wide, s32[2,4,2,16,128]{4,3,2,1,0:T(8,128)S(1)} %pad_add_fusion.bins_own, s32[2,4,2,16,128]{4,3,2,1,0:T(8,128)S(1)} %collective-permute-done.8.bins_other, f32[4,80,128]{2,1,0:T(8,128)S(1)} %get-tuple-element.12.before), custom_call_target="tpu_custom_call" | custom-call | flops 13631488 | bytes 860160 | tf_op jit(solution)/shard_map/pallas_call | solution.py:246
  19.7 0.0 collective-permute-done.11.bins_other
  19.7 3.5 %shard_map.49 = (f32[96,128]{1,0:T(8,128)S(1)}, f32[96,128]{1,0:T(8,128)S(1)}) custom-call(f32[26,8,128]{2,1,0:T(8,128)S(1)} %get-tuple-element.11.wide, s32[2,4,2,16,128]{4,3,2,1,0:T(8,128)S(1)} %pad_add_fusion.1.bins_own, s32[2,4,2,16,128]{4,3,2,1,0:T(8,128)S(1)} %collective-permute-done.11.bins_other, f32[4,80,128]{2,1,0:T(8,128)S(1)} %shard_map.48.before), custom_call_target="tpu_custom_call" | custom-call | flops 27262976 | bytes 958464 | tf_op jit(solution)/shard_map/pallas_call | solution.py:246
  23.2 0.4 %collective-permute-start.12 = (f32[96,128]{1,0:T(8,128)S(1)}, f32[96,128]{1,0:T(8,128)S(1)}, u32[]{:S(2)}, u32[]{:S(2)}) collective-permute-start(f32[96,128]{1,0:T(8,128)S(1)} %get-tuple-element.14), channel_id=1, source_target_pairs={{0,1},{1,0},{2,3},{3,2},{4,5},{5,4},{6,7},{7,6},{8,9},{9,8},{10,11... | collective-permute-start | bytes 147464 | tf_op jit(solution)/shard_map/ppermute | solution.py:45
  23.6 0.9 %collective-permute-done.12.other = f32[96,128]{1,0:T(8,128)S(1)} collective-permute-done((f32[96,128]{1,0:T(8,128)S(1)}, f32[96,128]{1,0:T(8,128)S(1)}, u32[]{:S(2)}, u32[]{:S(2)}) %collective-permute-start.12) | collective-permute-done | bytes 49184 | tf_op jit(solution)/shard_map/ppermute | solution.py:45
  24.5 1.4 %imaging.1 = f32[1,16,16,128]{3,2,1,0:T(8,128)} custom-call(s32[2,16]{1,0:T(2,128)S(1)} %get-tuple-element.10.offsets, f32[96,128]{1,0:T(8,128)S(1)} %get-tuple-element.13.mine, f32[96,128]{1,0:T(8,128)S(1)} %collective-permute-done.12.other), custom_call_target="tpu_custom_call" | custom-call | tf_op jit(solution)/shard_map/imaging/pallas_call | solution.py:339
  (13 shorter events, 0.1 us)
Async XLA Ops:
  0.0 5.0 %collective-permute-start.2 = (s32[1,2,16,128]{3,2,1,0:T(8,128)}, s32[1,2,16,128]{3,2,1,0:T(8,128)S(1)}, u32[]{:S(2)}, u32[]{:S(2)}) collective-permute-start(s32[1,2,16,128]{3,2,1,0:T(8,128)} %bins.1), channel_id=1, source_target_pairs={{0,17},{1,16},{2,19},{3,18},{4,21},{5,20},{6,23},{7,22},{8,25},{9,... | collective-permute-start | bytes 49160 | tf_op jit(solution)/shard_map/ppermute | solution.py:45
  0.6 4.6 %collective-permute-start.3 = (s32[1,2,16,128]{3,2,1,0:T(8,128)}, s32[1,2,16,128]{3,2,1,0:T(8,128)S(1)}, u32[]{:S(2)}, u32[]{:S(2)}) collective-permute-start(s32[1,2,16,128]{3,2,1,0:T(8,128)} %bins.1), channel_id=1, source_target_pairs={{0,24},{1,25},{2,26},{3,27},{4,28},{5,29},{6,30},{7,31},{8,16},{9,... | collective-permute-start | bytes 49160 | tf_op jit(solution)/shard_map/ppermute | solution.py:45
  2.8 5.0 %collective-permute-start.4 = (s32[1,2,16,128]{3,2,1,0:T(8,128)}, s32[1,2,16,128]{3,2,1,0:T(8,128)S(1)}, u32[]{:S(2)}, u32[]{:S(2)}) collective-permute-start(s32[1,2,16,128]{3,2,1,0:T(8,128)} %bins.1), channel_id=1, source_target_pairs={{0,9},{1,8},{2,11},{3,10},{4,13},{5,12},{6,15},{7,14},{8,1},{9,0},... | collective-permute-start | bytes 49160 | tf_op jit(solution)/shard_map/ppermute | solution.py:45
  3.2 9.5 %collective-permute-start = (f32[1,4,2,16,128]{4,3,2,1,0:T(8,128)}, f32[1,4,2,16,128]{4,3,2,1,0:T(8,128)S(1)}, u32[]{:S(2)}, u32[]{:S(2)}) collective-permute-start(f32[1,4,2,16,128]{4,3,2,1,0:T(8,128)} %bitcast.11), channel_id=1, source_target_pairs={{0,3},{1,2},{2,1},{3,0},{4,7},{5,6},{6,5},{7,4},{8,11},{9,10},{10,... | collective-permute-start | bytes 196616 | tf_op jit(solution)/shard_map/ppermute | solution.py:45
  3.7 0.7 %copy-start.1 = (s32[1,2,16,128]{3,2,1,0:T(8,128)S(1)}, s32[1,2,16,128]{3,2,1,0:T(8,128)}, u32[]{:S(2)}) copy-start(s32[1,2,16,128]{3,2,1,0:T(8,128)} %bins.1) | copy-start | bytes 49156
  5.2 4.7 %collective-permute-start.6 = (s32[2,2,16,128]{3,2,1,0:T(8,128)S(1)}, s32[2,2,16,128]{3,2,1,0:T(8,128)S(1)}, u32[]{:S(2)}, u32[]{:S(2)}) collective-permute-start(s32[2,2,16,128]{3,2,1,0:T(8,128)S(1)} %constant_dynamic-update-slice_fusion), channel_id=1, source_target_pairs={{0,3},{1,2},{2,1},{3,0},{4,7},{5,6},{6,5},{7,4},{8,11},{9,10},{10,... | collective-permute-start | bytes 98312 | tf_op jit(solution)/shard_map/ppermute | solution.py:45
  6.6 4.2 %collective-permute-start.7 = (s32[2,2,16,128]{3,2,1,0:T(8,128)S(1)}, s32[2,2,16,128]{3,2,1,0:T(8,128)S(1)}, u32[]{:S(2)}, u32[]{:S(2)}) collective-permute-start(s32[2,2,16,128]{3,2,1,0:T(8,128)S(1)} %constant_dynamic-update-slice_fusion), channel_id=1, source_target_pairs={{0,6},{1,7},{2,4},{3,5},{4,2},{5,3},{6,0},{7,1},{8,14},{9,15},{10,... | collective-permute-start | bytes 98312 | tf_op jit(solution)/shard_map/ppermute | solution.py:45
  7.8 4.3 %collective-permute-start.10 = (s32[2,2,16,128]{3,2,1,0:T(8,128)S(1)}, s32[2,2,16,128]{3,2,1,0:T(8,128)S(1)}, u32[]{:S(2)}, u32[]{:S(2)}) collective-permute-start(s32[2,2,16,128]{3,2,1,0:T(8,128)S(1)} %pad_add_fusion.4), channel_id=1, source_target_pairs={{0,6},{1,7},{2,4},{3,5},{4,2},{5,3},{6,0},{7,1},{8,14},{9,15},{10,... | collective-permute-start | bytes 98312 | tf_op jit(solution)/shard_map/ppermute | solution.py:45
  9.0 3.7 %collective-permute-start.9 = (s32[2,2,16,128]{3,2,1,0:T(8,128)S(1)}, s32[2,2,16,128]{3,2,1,0:T(8,128)S(1)}, u32[]{:S(2)}, u32[]{:S(2)}) collective-permute-start(s32[2,2,16,128]{3,2,1,0:T(8,128)S(1)} %pad_add_fusion.4), channel_id=1, source_target_pairs={{0,3},{1,2},{2,1},{3,0},{4,7},{5,6},{6,5},{7,4},{8,11},{9,10},{10,... | collective-permute-start | bytes 98312 | tf_op jit(solution)/shard_map/ppermute | solution.py:45
  9.9 4.7 %collective-permute-start.5 = (s32[4,2,16,128]{3,2,1,0:T(8,128)S(1)}, s32[4,2,16,128]{3,2,1,0:T(8,128)S(1)}, u32[]{:S(2)}, u32[]{:S(2)}) collective-permute-start(s32[4,2,16,128]{3,2,1,0:T(8,128)S(1)} %pad_add_fusion.2), channel_id=1, source_target_pairs={{0,5},{1,4},{2,7},{3,6},{4,1},{5,0},{6,3},{7,2},{8,13},{9,12},{10,... | collective-permute-start | bytes 196616 | tf_op jit(solution)/shard_map/ppermute | solution.py:45
  10.8 1.9 %copy-start.3 = (f32[2,2,2,16,128]{4,3,2,1,0:T(8,128)S(1)}, f32[2,2,2,16,128]{4,3,2,1,0:T(8,128)}, u32[]{:S(2)}) copy-start(f32[2,2,2,16,128]{4,3,2,1,0:T(8,128)} %param.4) | copy-start | bytes 196612
  12.7 2.6 %collective-permute-start.1 = (f32[2,4,2,16,128]{4,3,2,1,0:T(8,128)S(1)}, f32[2,4,2,16,128]{4,3,2,1,0:T(8,128)S(1)}, u32[]{:S(2)}, u32[]{:S(2)}) collective-permute-start(f32[2,4,2,16,128]{4,3,2,1,0:T(8,128)S(1)} %pad_maximum_fusion.surf_own), channel_id=1, source_target_pairs={{0,1},{1,0},{2,3},{3,2},{4,5},{5,4},{6,7},{7,6},{8,9},{9,8},{10,11... | collective-permute-start | bytes 393224 | tf_op jit(solution)/shard_map/ppermute | solution.py:45
  14.7 1.5 %collective-permute-start.8 = (s32[2,4,2,16,128]{4,3,2,1,0:T(8,128)S(1)}, s32[2,4,2,16,128]{4,3,2,1,0:T(8,128)S(1)}, u32[]{:S(2)}, u32[]{:S(2)}) collective-permute-start(s32[2,4,2,16,128]{4,3,2,1,0:T(8,128)S(1)} %pad_add_fusion.bins_own), channel_id=1, source_target_pairs={{0,1},{1,0},{2,3},{3,2},{4,5},{5,4},{6,7},{7,6},{8,9},{9,8},{10,11... | collective-permute-start | bytes 393224 | tf_op jit(solution)/shard_map/ppermute | solution.py:45
  15.2 1.0 %copy-start = (f32[13,2,2,128]{3,2,1,0:T(2,128)S(1)}, f32[13,2,2,128]{3,2,1,0:T(2,128)}, u32[]{:S(2)}) copy-start(f32[13,2,2,128]{3,2,1,0:T(2,128)} %table.1) | copy-start | bytes 79876
  15.2 1.0 %copy-start.2 = (s32[16,2]{0,1:T(2,128)S(1)}, s32[16,2]{0,1:T(2,128)}, u32[]{:S(2)}) copy-start(s32[16,2]{0,1:T(2,128)} %param.7) | copy-start | bytes 388
  15.2 4.5 %collective-permute-start.11 = (s32[2,4,2,16,128]{4,3,2,1,0:T(8,128)S(1)}, s32[2,4,2,16,128]{4,3,2,1,0:T(8,128)S(1)}, u32[]{:S(2)}, u32[]{:S(2)}) collective-permute-start(s32[2,4,2,16,128]{4,3,2,1,0:T(8,128)S(1)} %pad_add_fusion.1.bins_own), channel_id=1, source_target_pairs={{0,1},{1,0},{2,3},{3,2},{4,5},{5,4},{6,7},{7,6},{8,9},{9,8},{10,11... | collective-permute-start | bytes 393224 | tf_op jit(solution)/shard_map/ppermute | solution.py:45
  23.2 1.3 %collective-permute-start.12 = (f32[96,128]{1,0:T(8,128)S(1)}, f32[96,128]{1,0:T(8,128)S(1)}, u32[]{:S(2)}, u32[]{:S(2)}) collective-permute-start(f32[96,128]{1,0:T(8,128)S(1)} %get-tuple-element.14), channel_id=1, source_target_pairs={{0,1},{1,0},{2,3},{3,2},{4,5},{5,4},{6,7},{7,6},{8,9},{9,8},{10,11... | collective-permute-start | bytes 147464 | tf_op jit(solution)/shard_map/ppermute | solution.py:45
